TPU v7x, 256 devices: a whole 4x4x8 slice. The times are simulated.
256 devices in a mesh: member: 8 (over x, z_hi), rows: 32 (over y, z_lo, core).
Axes of the slice: x: 4, y: 4, z: 8 (z_hi: 2, z_lo: 4; z = z_hi * 4 + z_lo), core: 2. Of those that a mesh axis runs over, the one named last changes fastest.
Arguments:
- member_latent_state: bfloat16 [16, 128, 64, 512], P('member', 'rows'), as said below
- analysis_target_field: bfloat16 [128, 64, 512], P('rows'), may hold values from -8 to 8
- conv_first: bfloat16 [512, 9, 512], replicated, may hold values from -0.09375 to 0.09375
- second_kernel_weight: bfloat16 [512, 9, 512], replicated, may hold values from -0.09375 to 0.09375
Outputs:
- ensemble_prognosis_field: bfloat16 [16, 128, 64, 512], P('member', 'rows')
- initial_conv_derivative: float32 [512, 9, 512], P('rows')
- final_filter_slope: float32 [512, 9, 512], P('rows')
Inputs may be any that keep to these rules, and one draw needn't show every extreme that they name: `member_latent_state`: each member's field is drawn independently.
All inputs are finite; a program needn't handle non-finite values.
Results may differ from a plain program's by a relative error of at most 0.0058.
Values may be sent and summed in bfloat16 or wider, within the bound.
A program may use at most 192 MiB of HBM per device.

v0:
```python
import jax
import jax.numpy as jnp
from jax import lax
from jax.sharding import PartitionSpec as P

SOFTENING_EPS = 0.1
INV_ROOT_TWO = 0.7071067811865476
INV_ROOT_TWOPI = 0.3989422804014327


def padded_2(block, sides, width):
    for axis, dim in sides:
        count = lax.axis_size(axis)
        forward = [(i, i + 1) for i in range(count - 1)]
        backward = [(target, source) for source, target in forward]
        low = lax.ppermute(
            lax.slice_in_dim(block, block.shape[dim] - width, None, axis=dim), axis, forward
        )
        high = lax.ppermute(lax.slice_in_dim(block, 0, width, axis=dim), axis, backward)
        block = jnp.concatenate([low, block, high], axis=dim)
    return block


def gelu_value(pre):
    return 0.5 * pre * (1.0 + lax.erf(pre * INV_ROOT_TWO))


def gelu_slope(pre):
    return (
        0.5 * (1.0 + lax.erf(pre * INV_ROOT_TWO)) + pre * jnp.exp(-0.5 * pre * pre) * INV_ROOT_TWOPI
    )


def pad_columns(field):
    return jnp.pad(field, ((0, 0), (0, 0), (1, 1), (0, 0)))


def slab_padded(field):
    extended = padded_2(field, (("rows", 1),), 1)
    return pad_columns(extended)


def haloed_adjoint(field):
    extended = padded_2(field, (("rows", 1),), 1)
    return pad_columns(extended)


def tap_view(padded, tap_index, meridian_extent, longitude_length):
    down = tap_index // 3
    across = tap_index % 3
    return padded[:, down : down + meridian_extent, across : across + longitude_length, :]


def apply_kernel_stencil(padded, kernel, meridian_extent, longitude_length):
    channels = padded.shape[3]
    summed = jnp.zeros(
        (padded.shape[0] * meridian_extent * longitude_length, kernel.shape[2]), jnp.float32
    )
    for tap_index in range(9):
        view = tap_view(padded, tap_index, meridian_extent, longitude_length).reshape(-1, channels)
        summed = summed + jnp.dot(view, kernel[:, tap_index, :], preferred_element_type=jnp.float32)
    return summed.reshape(padded.shape[0], meridian_extent, longitude_length, kernel.shape[2])


def reversed_stencil(padded, kernel, meridian_extent, longitude_length):
    channels = padded.shape[3]
    summed = jnp.zeros(
        (padded.shape[0] * meridian_extent * longitude_length, kernel.shape[0]), jnp.float32
    )
    for tap_index in range(9):
        view = tap_view(padded, 8 - tap_index, meridian_extent, longitude_length).reshape(
            -1, channels
        )
        summed = summed + lax.dot_general(
            view,
            kernel[:, tap_index, :],
            (((1,), (1,)), ((), ())),
            preferred_element_type=jnp.float32,
        )
    return summed.reshape(padded.shape[0], meridian_extent, longitude_length, kernel.shape[0])


def tap_terms(padded, flat_cot, meridian_extent, longitude_length):
    channels = padded.shape[3]
    taps_list = []
    for tap_index in range(9):
        view = tap_view(padded, tap_index, meridian_extent, longitude_length).reshape(-1, channels)
        taps_list.append(
            lax.dot_general(
                view, flat_cot, (((0,), (0,)), ((), ())), preferred_element_type=jnp.float32
            )
        )
    return jnp.stack(taps_list, axis=1)


def stencil_derivative(padded, cotangent, meridian_extent, longitude_length):
    flat_cot = cotangent.reshape(-1, cotangent.shape[3])
    own_share = lax.psum_scatter(
        tap_terms(padded, flat_cot, meridian_extent, longitude_length),
        "rows",
        scatter_dimension=0,
        tiled=True,
    )
    return lax.psum(own_share, "member")


def attraction_sum(local, everyone):

    def step(running, other):
        spread = local - other[None]
        smooth_abs = jnp.sqrt(spread * spread + SOFTENING_EPS * SOFTENING_EPS)
        return (running + spread / smooth_abs, None)

    result, unused = lax.scan(step, jnp.zeros(local.shape, jnp.float32), everyone)
    return result


def predicted_gradient(
    model_output_field,
    measured_truth_field,
    pairwise_spread_part,
    ensemble_draw_count,
    row_sum_complete,
):
    prognosis_misfit = model_output_field - measured_truth_field
    distance_to_analysis = jnp.sqrt(
        prognosis_misfit * prognosis_misfit + SOFTENING_EPS * SOFTENING_EPS
    )
    return (
        prognosis_misfit / distance_to_analysis / ensemble_draw_count
        - pairwise_spread_part / (ensemble_draw_count * (ensemble_draw_count - 1.0))
    ) / row_sum_complete


def body(member_latent_state, analysis_target_field, conv_first, second_kernel_weight):
    meridian_extent = member_latent_state.shape[1]
    longitude_length = member_latent_state.shape[2]
    ensemble_draw_count = float(member_latent_state.shape[0] * lax.axis_size("member"))
    row_sum_complete = float(meridian_extent * lax.axis_size("rows"))
    padded_state = slab_padded(member_latent_state)
    pre_first = apply_kernel_stencil(padded_state, conv_first, meridian_extent, longitude_length)
    hidden = gelu_value(pre_first).astype(jnp.bfloat16)
    hidden_state_bordered = slab_padded(hidden)
    model_output_field = member_latent_state.astype(jnp.float32) + apply_kernel_stencil(
        hidden_state_bordered, second_kernel_weight, meridian_extent, longitude_length
    )
    ensemble_prognosis_field = model_output_field.astype(jnp.bfloat16)
    pairwise_spread_part = attraction_sum(
        model_output_field, lax.all_gather(model_output_field, "member", axis=0, tiled=True)
    )
    measured_truth_field = analysis_target_field.astype(jnp.float32)[None]
    activation_gradient_factor = predicted_gradient(
        model_output_field,
        measured_truth_field,
        pairwise_spread_part,
        ensemble_draw_count,
        row_sum_complete,
    )
    output_cotangent_field = activation_gradient_factor.astype(jnp.bfloat16)
    final_filter_slope = stencil_derivative(
        hidden_state_bordered, output_cotangent_field, meridian_extent, longitude_length
    )
    intermediate_adjoint = reversed_stencil(
        haloed_adjoint(output_cotangent_field),
        second_kernel_weight,
        meridian_extent,
        longitude_length,
    )
    cot_pre = (intermediate_adjoint * gelu_slope(pre_first)).astype(jnp.bfloat16)
    initial_conv_derivative = stencil_derivative(
        padded_state, cot_pre, meridian_extent, longitude_length
    )
    return (ensemble_prognosis_field, initial_conv_derivative, final_filter_slope)


def solution(mesh):
    in_specs = (P("member", "rows", None, None), P("rows", None, None), P(), P())
    out_specs = (P("member", "rows", None, None), P("rows", None, None), P("rows", None, None))
    return jax.shard_map(body, mesh=mesh, in_specs=in_specs, out_specs=out_specs, check_vma=False)
```

profile of v0, /device:TPU:1, one launch (start us, length us, event | category | flops | bytes accessed | tf_op | source)
XLA Modules:
  0.0 728.0 jit_solution(73099665500884084)
XLA Ops:
  8.4 5.1 collective-permute-start
  13.5 1.9 collective-permute-start.1
  16.6 3.3 collective-permute-done.1
  26.0 2.2 collective-permute-start.2
  28.2 2.5 collective-permute-start.3
  30.8 5.5 collective-permute-done.3
  42.6 1.8 convert_element_type.29
  44.4 176.7 %all-gather.2.cloned.1.call-done = f32[16,4,64,512]{3,2,1,0:T(8,128)} async-done(((f32[2,4,64,512]{3,2,1,0:T(8,128)}), f32[16,4,64,512]{3,2,1,0:T(8,128)}) %all-gather.2.cloned.1.call-update) | async-done | bytes 8388624 | tf_op jit(solution)/shard_map/all_gather | solution.py:149
  221.1 47.6 %while.11 = (s32[]{:T(128)}, f32[2,4,64,512]{3,2,1,0:T(8,128)S(1)}, f32[16,4,64,512]{3,2,1,0:T(8,128)}, f32[2,4,64,512]{3,2,1,0:T(8,128)}, s32[]{:T(128)}, /*index=5*/s32[]{:T(128)}) while((s32[]{:T(128)}, f32[2,4,64,512]{3,2,1,0:T(8,128)S(1)}, f32[16,4,64,512]{3,2,1,0:T(8,128)}, f32[2,4,64,512]{3,2,1,0:T(8,128)}, s32[]{:T(128)}, ...), condition=%wide.region_1.2_spmd.clone, body=%wide.region_0.1_spmd.clone.sunk | while | flops 1572867 | bytes 4718683 | solution.py:114
  222.2 1.9 select_add_fusion.2
  225.1 1.9 select_add_fusion.2
  228.1 1.9 select_add_fusion.2
  231.1 1.9 select_add_fusion.2
  234.1 1.9 select_add_fusion.2
  237.0 1.9 select_add_fusion.2
  240.0 1.9 select_add_fusion.2
  243.0 1.9 select_add_fusion.2
  246.0 1.9 select_add_fusion.2
  249.0 1.9 select_add_fusion.2
  251.9 1.9 select_add_fusion.2
  254.9 1.9 select_add_fusion.2
  257.9 1.9 select_add_fusion.2
  260.9 1.9 select_add_fusion.2
  263.8 1.9 select_add_fusion.2
  266.8 1.9 select_add_fusion.2
  268.7 1.8 multiply_convert_fusion
  270.5 1.4 fusion.11
  273.4 1.5 fusion.10
  274.9 1.4 fusion.9
  277.7 1.5 fusion.7
  279.2 1.5 fusion.6
  280.7 1.5 fusion.1
  282.2 1.5 fusion.5
  284.7 2.4 collective-permute-start.4
  287.1 2.1 collective-permute-start.5
  289.2 8.9 %collective-permute-done.5 = bf16[2,1,64,512]{3,2,1,0:T(8,128)(2,1)S(1)} collective-permute-done((bf16[2,1,64,512]{3,2,1,0:T(8,128)(2,1)S(1)}, bf16[2,1,64,512]{3,2,1,0:T(8,128)(2,1)S(1)}, u32[]{:S(2)}, u32[]{:S(2)}) %collective-permute-start.5) | collective-permute-done | bytes 131104 | tf_op jit(solution)/shard_map/ppermute | solution.py:19
  299.0 1.9 fusion.57
  305.2 1.5 fusion.18
  306.7 1.4 fusion.4
  309.5 1.4 fusion.16
  311.0 1.5 fusion.15
  312.5 1.4 fusion.14
  315.3 1.5 fusion.3
  318.3 121.6 %reduce-scatter.5.cloned.1.call-done = f32[16,9,512]{2,0,1:T(8,128)} async-done(((f32[512,9,512]{2,0,1:T(8,128)}), f32[16,9,512]{2,0,1:T(8,128)}) %reduce-scatter.5.cloned.1.call-update) | async-done | bytes 294928 | tf_op jit(solution)/shard_map/reduce_scatter | solution.py:98
  440.0 163.7 %reduce-scatter.3.cloned.1.call-done = f32[16,9,512]{2,0,1:T(8,128)} async-done(((f32[512,9,512]{2,0,1:T(8,128)}), f32[16,9,512]{2,0,1:T(8,128)}) %reduce-scatter.3.cloned.1.call-update) | async-done | bytes 294928 | tf_op jit(solution)/shard_map/reduce_scatter | solution.py:98
  603.7 114.4 %all-reduce.6.cloned.1.call-done = (f32[16,9,512]{2,0,1:T(8,128)}, f32[16,9,512]{2,0,1:T(8,128)}) async-done(((f32[16,9,512]{2,0,1:T(8,128)}, f32[16,9,512]{2,0,1:T(8,128)}), (f32[16,9,512]{2,0,1:T(8,128)}, f32[16,9,512]{2,0,1:T(8,128)})) %all-reduce.6.cloned.1.call-update) | async-done | bytes 589840 | tf_op jit(solution)/shard_map/psum | solution.py:104
  718.1 1.7 copy.54
  719.8 1.7 copy.55
  (119 shorter events, 45.1 us)
Async XLA Ops:
  7.2 13.6 %copy-start.2 = (bf16[2,4,64,512]{3,2,1,0:T(8,128)(2,1)S(1)}, bf16[2,4,64,512]{3,2,1,0:T(8,128)(2,1)}, u32[]{:S(2)}) copy-start(bf16[2,4,64,512]{3,2,1,0:T(8,128)(2,1)} %param.6) | copy-start | bytes 1572868
  7.2 213.9 %all-gather.2.cloned.1.call-start = ((), (), s32[]{:S(2)}) async-start(), calls=%async_computation.2 | async-start | bytes 9437184 | tf_op jit(solution)/shard_map/all_gather | solution.py:149
  7.2 14.2 %slice-start.4 = ((s8[4718592]{0:T(1024)(128)(4,1)}), s8[4194304]{0:T(1024)(128)(4,1)S(1)}, s32[]{:S(2)}) async-start(s8[4718592]{0:T(1024)(128)(4,1)} %bitcast.305), calls=%async_computation.10 | async-start | bytes 8388608
  8.4 7.0 collective-permute-start
  13.5 6.4 collective-permute-start.1
  16.6 4.2 copy-start.9
  19.8 0.8 copy-start.7
  20.7 1.0 slice-start.5
  25.3 11.6 %slice-start = ((s8[4718592]{0:T(1024)(128)(4,1)}), s8[4194304]{0:T(1024)(128)(4,1)S(1)}, s32[]{:S(2)}) async-start(s8[4718592]{0:T(1024)(128)(4,1)} %bitcast.297), calls=%async_computation.6 | async-start | bytes 8388608
  25.8 13.1 %copy-start = (f32[512,512]{1,0:T(8,128)}, f32[512,512]{1,0:T(8,128)S(1)}, u32[]{:S(2)}) copy-start(f32[512,512]{1,0:T(8,128)S(1)} %fusion.21) | copy-start | bytes 3145732
  26.0 11.4 %copy-start.5 = (bf16[2,4,64,512]{3,2,1,0:T(8,128)(2,1)}, bf16[2,4,64,512]{3,2,1,0:T(8,128)(2,1)S(1)}, u32[]{:S(2)}) copy-start(bf16[2,4,64,512]{3,2,1,0:T(8,128)(2,1)S(1)} %multiply_convert_fusion.2) | copy-start | bytes 1572868
  26.0 4.8 collective-permute-start.2
  28.2 8.7 %slice-start.1 = ((s8[4718592]{0:T(1024)(128)(4,1)}), s8[524288]{0:T(1024)(128)(4,1)S(1)}, s32[]{:S(2)}) async-start(s8[4718592]{0:T(1024)(128)(4,1)} %bitcast.297), calls=%async_computation.7 | async-start | bytes 1048576
  28.2 8.0 %collective-permute-start.3 = (bf16[2,1,64,512]{3,2,1,0:T(8,128)(2,1)S(1)}, bf16[2,1,64,512]{3,2,1,0:T(8,128)(2,1)S(1)}, u32[]{:S(2)}, u32[]{:S(2)}) collective-permute-start(bf16[2,1,64,512]{3,2,1,0:T(8,128)(2,1)S(1)} %get-tuple-element.78), channel_id=1, source_target_pairs={{1,0},{2,1},{3,2},{4,3},{5,4},{6,5},{7,6},{8,7},{9,8},{10,9},{11,1... | collective-permute-start | bytes 393224 | tf_op jit(solution)/shard_map/ppermute | solution.py:19
  30.8 6.6 copy-start.11
  42.5 397.5 %reduce-scatter.5.cloned.1.call-start = ((), (), s32[]{:S(2)}) async-start(), calls=%async_computation.4 | async-start | bytes 9732096 | tf_op jit(solution)/shard_map/reduce_scatter | solution.py:98
  268.7 3.2 copy-start.6
  268.7 3.2 copy-start.12
  270.5 11.6 %copy-start.3 = (bf16[2,4,64,512]{3,2,1,0:T(8,128)(2,1)}, bf16[2,4,64,512]{3,2,1,0:T(8,128)(2,1)S(1)}, u32[]{:S(2)}) copy-start(bf16[2,4,64,512]{3,2,1,0:T(8,128)(2,1)S(1)} %multiply_convert_fusion) | copy-start | bytes 1572868
  283.6 1.0 copy-start.4
  283.6 320.0 %reduce-scatter.3.cloned.1.call-start = ((), (), s32[]{:S(2)}) async-start(), calls=%async_computation.3 | async-start | bytes 9732096 | tf_op jit(solution)/shard_map/reduce_scatter | solution.py:98
  284.7 4.6 collective-permute-start.4
  287.1 11.0 %collective-permute-start.5 = (bf16[2,1,64,512]{3,2,1,0:T(8,128)(2,1)S(1)}, bf16[2,1,64,512]{3,2,1,0:T(8,128)(2,1)S(1)}, u32[]{:S(2)}, u32[]{:S(2)}) collective-permute-start(bf16[2,1,64,512]{3,2,1,0:T(8,128)(2,1)S(1)} %get-tuple-element.74), channel_id=1, source_target_pairs={{1,0},{2,1},{3,2},{4,3},{5,4},{6,5},{7,6},{8,7},{9,8},{10,9},{11,1... | collective-permute-start | bytes 393224 | tf_op jit(solution)/shard_map/ppermute | solution.py:19
  298.2 2.6 slice-start.2
  298.5 2.4 slice-start.3
  303.3 1.5 copy-start.1
  304.3 2.4 copy-start.10
  311.0 4.4 copy-start.8
  318.3 399.8 %all-reduce.6.cloned.1.call-start = ((), (), s32[]{:S(2)}) async-start(), calls=%async_computation.5 | async-start | bytes 1179648 | tf_op jit(solution)/shard_map/psum | solution.py:104
Sparse Core Ops, SparseCore 0:
  42.6 178.4 all-gather.1
  283.8 156.1 reduce-scatter.4
  442.5 161.0 reduce-scatter.2
  606.2 111.8 all-reduce.5
where the time goes:
time: 736 us; the launch traced here: 728 us
  waiting for transfers between devices  594 us (81%)
  matrix products  39.7 us (5%)
  other arithmetic  36.4 us (5%)
  local copies, waits for them, and re-layouts  26.6 us (4%)
  starting transfers between devices  16.4 us (2%)
  between operations  14.4 us (2%)
    reduce_scatter x2, waiting for transfers between devices, stencil_derivative(): lax.psum_scatter(tap_terms(padded, flat_cot, meridian_extent, longitude_l...  285 us
    all_gather x1, waiting for transfers between devices, body(): lax.all_gather(model_output_field, 'member', axis=0, tiled=True)  177 us
    psum x1, waiting for transfers between devices, stencil_derivative(): return lax.psum(own_share, 'member')  114 us
    add x16, other arithmetic, step(): return (running + spread / smooth_abs, None)  30 us
    dot_general x18, matrix products, tap_terms(): lax.dot_general(view, flat_cot, (((0,), (0,)), ((), ())), preferred_eleme...  26.2 us
    ppermute x3, waiting for transfers between devices, padded_2(): lax.ppermute(lax.slice_in_dim(block, 0, width, axis=dim), axis, backward)  17.6 us
    sub x16, local copies, waits for them, and re-layouts, step(): spread = local - other[None]  17.3 us
  transfers between devices with their start and end apart: 10, of which 7 were waited for; matrix products, arithmetic and copies ran while one was open for 3% of the time, Pallas kernels for 0%

commit v1 on v0

v1 whole, which is shorter than its diff:
```python
import functools

import jax
import jax.numpy as jnp
from jax import lax
from jax.experimental import pallas as pl
from jax.experimental.pallas import tpu as pltpu
from jax.sharding import PartitionSpec as P

MESH = pl.DeviceIdType.MESH
EPS2 = 0.1 * 0.1
INV_ROOT_TWO = 0.7071067811865476
INV_ROOT_TWOPI = 0.3989422804014327


def gelu_value(pre):
    return 0.5 * pre * (1.0 + lax.erf(pre * INV_ROOT_TWO))


def gelu_slope(pre):
    return 0.5 * (1.0 + lax.erf(pre * INV_ROOT_TWO)) + pre * jnp.exp(-0.5 * pre * pre) * INV_ROOT_TWOPI


def padded(field):
    count = lax.axis_size("rows")
    forward = [(i, i + 1) for i in range(count - 1)]
    backward = [(b, a) for a, b in forward]
    low = lax.ppermute(field[:, -1:], "rows", forward)
    high = lax.ppermute(field[:, :1], "rows", backward)
    field = jnp.concatenate([low, field, high], axis=1)
    return jnp.pad(field, ((0, 0), (0, 0), (1, 1), (0, 0)))


def tap_view(pad, tap, rows, cols):
    return pad[:, tap // 3 : tap // 3 + rows, tap % 3 : tap % 3 + cols, :].reshape(-1, pad.shape[3])


def conv(pad, kernel, rows, cols):
    total = 0.0
    for tap in range(9):
        total = total + jnp.dot(tap_view(pad, tap, rows, cols), kernel[:, tap, :], preferred_element_type=jnp.float32)
    return total.reshape(pad.shape[0], rows, cols, kernel.shape[2])


def adjoint(pad, kernel, rows, cols):
    total = 0.0
    for tap in range(9):
        total = total + lax.dot_general(
            tap_view(pad, 8 - tap, rows, cols),
            kernel[:, tap, :],
            (((1,), (1,)), ((), ())),
            preferred_element_type=jnp.float32,
        )
    return total.reshape(pad.shape[0], rows, cols, kernel.shape[0])


def tap_terms(pad, cot, rows, cols):
    flat = cot.reshape(-1, cot.shape[3])
    terms = []
    for tap in range(9):
        terms.append(
            lax.dot_general(
                tap_view(pad, tap, rows, cols), flat, (((0,), (0,)), ((), ())), preferred_element_type=jnp.float32
            ).astype(jnp.bfloat16)
        )
    return jnp.stack(terms, axis=0)


SUB = 2


def score_kernel(f_ref, t_ref, out_ref, everyone, cots, s1, r1, s2, r2):
    member, rows = lax.axis_index("member"), lax.axis_index("rows")
    cells = everyone.shape[1]
    width = cells // SUB

    def peer(k):
        return {"member": lax.rem(member + k, 8), "rows": rows}

    barrier = pltpu.get_barrier_semaphore()
    for k in range(1, 8):
        pl.semaphore_signal(barrier, inc=1, device_id=peer(k), device_id_type=MESH)
    pl.semaphore_wait(barrier, 7)

    def out_copy(s, k):
        to = lax.rem(member + k, 8)
        start = pl.multiple_of(to * cells + s * width, 8)
        return pltpu.make_async_remote_copy(
            src_ref=f_ref.at[:, pl.ds(start, width)],
            dst_ref=everyone.at[pl.ds(member * 2, 2), pl.ds(s * width, width)],
            send_sem=s1.at[s, k],
            recv_sem=r1.at[s, k],
            device_id=peer(k),
            device_id_type=MESH,
        )

    def back_copy(s, k):
        to = lax.rem(member + k, 8)
        start = pl.multiple_of(member * cells + s * width, 8)
        return pltpu.make_async_remote_copy(
            src_ref=cots.at[pl.ds(to * 2, 2), pl.ds(s * width, width)],
            dst_ref=out_ref.at[:, pl.ds(start, width)],
            send_sem=s2.at[s, k],
            recv_sem=r2.at[s, k],
            device_id=peer(k),
            device_id_type=MESH,
        )

    for s in range(SUB):
        for k in (4, 3, 5, 1, 7, 2, 6):
            out_copy(s, k).start()
    mine = pl.multiple_of(member * cells, 8)
    everyone[pl.ds(member * 2, 2)] = f_ref[:, pl.ds(mine, cells)]
    for s in range(SUB):
        for k in range(1, 8):
            out_copy(s, k).wait_recv()

        @pl.loop(0, width // 16)
        def _(c):
            start = pl.multiple_of(s * width + c * 16, 16)
            tstart = pl.multiple_of(mine + s * width + c * 16, 16)
            for lane in range(0, 512, 128):
                spot = (pl.ds(start, 16), pl.ds(lane, 128))
                truth = t_ref[pl.ds(tstart, 16), pl.ds(lane, 128)].astype(jnp.float32)
                xs = [everyone[(k,) + spot] for k in range(16)]
                pulls = [None] * 16

                def plus(i, v):
                    pulls[i] = v if pulls[i] is None else pulls[i] + v

                for a in range(16):
                    for b in range(a + 1, 16):
                        d = xs[a] - xs[b]
                        u = d * lax.rsqrt(d * d + EPS2)
                        plus(a, u)
                        plus(b, -u)
                for k in range(16):
                    d = xs[k] - truth
                    slope = d * lax.rsqrt(d * d + EPS2)
                    cots[(k,) + spot] = (slope * (1.0 / 2048.0) - pulls[k] * (1.0 / 30720.0)).astype(jnp.bfloat16)

        for k in (4, 3, 5, 1, 7, 2, 6):
            back_copy(s, k).start()
    out_ref[:, pl.ds(mine, cells)] = cots[pl.ds(member * 2, 2)]
    for s in range(SUB):
        for k in range(1, 8):
            out_copy(s, k).wait_send()
            back_copy(s, k).wait()


def score(forecast, truth):
    members, cells, channels = forecast.shape
    part = cells // 8
    return pl.pallas_call(
        score_kernel,
        out_shape=jax.ShapeDtypeStruct(forecast.shape, jnp.bfloat16),
        in_specs=[pl.BlockSpec(memory_space=pltpu.VMEM)] * 2,
        out_specs=pl.BlockSpec(memory_space=pltpu.VMEM),
        scratch_shapes=[
            pltpu.VMEM((members * 8, part, channels), jnp.float32),
            pltpu.VMEM((members * 8, part, channels), jnp.bfloat16),
        ]
        + [pltpu.SemaphoreType.DMA((SUB, 8))] * 4,
        compiler_params=pltpu.CompilerParams(collective_id=0, has_side_effects=True, vmem_limit_bytes=32 << 20),
        name="score",
    )(forecast, truth)


def reduce_kernel(ga, gb, outa, outb, cr, sa, ra, sb, rb, ta, tra, tb, trb, u, ur, v, vr, fin, *sems):
    s0, r0, s1, r1, s2, r2, s3, r3, s4, r4, s5, r5 = sems
    member, rows = lax.axis_index("member"), lax.axis_index("rows")
    x, zh = member // 2, lax.rem(member, 2)
    y, z, c = rows // 8, lax.rem(rows // 2, 4), lax.rem(rows, 2)
    grads, outs = (ga, gb), (outa, outb)

    def at(px, pzh, py, pz, pc):
        return {"member": px * 2 + pzh, "rows": (py * 4 + pz) * 2 + pc}

    sibling = at(x, zh, y, z, 1 - c)
    far = at(x, 1 - zh, y, z, c)

    def along_y(k):
        return at(x, zh, lax.rem(y + k, 4), z, c)

    def along_x(k):
        return at(lax.rem(x + k, 4), zh, y, z, c)

    def along_z(k):
        return at(x, zh, y, lax.rem(z + k, 4), c)

    def send(src, dst, ssem, rsem, to):
        return pltpu.make_async_remote_copy(
            src_ref=src, dst_ref=dst, send_sem=ssem, recv_sem=rsem, device_id=to, device_id_type=MESH
        )

    barrier = pltpu.get_barrier_semaphore()
    peers = [sibling, far] + [a(k) for a in (along_y, along_x, along_z) for k in (1, 2, 3)]
    for p in peers:
        pl.semaphore_signal(barrier, inc=1, device_id=p, device_id_type=MESH)
    pl.semaphore_wait(barrier, len(peers))

    def step0(g):
        return send(grads[g].at[:, :, 1 - c], cr.at[g], s0.at[g], r0.at[g], sibling)

    def step1(g, h, k):
        s, r = (sa, ra) if h == 0 else (sb, rb)
        to = lax.rem((y if h == 0 else x) + k, 4)
        return send(
            s.at[g, to], r.at[g, k - 1], s1.at[g, h, k], r1.at[g, h, k], along_y(k) if h == 0 else along_x(k)
        )

    def step2(g, h, k):
        s, r = (ta, tra) if h == 0 else (tb, trb)
        to = lax.rem((x if h == 0 else y) + k, 4)
        return send(
            s.at[g, to], r.at[g, k - 1], s2.at[g, h, k], r2.at[g, h, k], along_x(k) if h == 0 else along_y(k)
        )

    def step3(g, k):
        to = lax.rem(z + k, 4)
        return send(u.at[g, to], ur.at[g, k - 1], s3.at[g, k], r3.at[g, k], along_z(k))

    def step4(g):
        return send(v.at[g], vr.at[g], s4.at[g], r4.at[g], far)

    def step5(g, k):
        return send(fin.at[g, x], fin.at[g, x], s5.at[g, k], r5.at[g, k], along_x(k))

    for g in range(2):
        step0(g).start()

    for g in range(2):
        step0(g).wait_recv()

        @pl.loop(0, 9)
        def _(tap):
            @pl.loop(0, 4)
            def _(yy):
                for zz in range(4):
                    block = grads[g][tap, yy * 4 + zz, c].astype(jnp.float32) + cr[g, tap, yy * 4 + zz].astype(
                        jnp.float32
                    )
                    block = block.astype(jnp.bfloat16)
                    for xx in range(4):
                        piece = block[:, xx * 128 : (xx + 1) * 128]
                        if zz < 2:
                            sa[g, yy, xx, tap, zz] = piece
                        else:
                            sb[g, xx, yy, tap, zz - 2] = piece

        for k in (2, 1, 3):
            step1(g, 0, k).start()
            step1(g, 1, k).start()

    def summed(own, got, where):
        total = own[where].astype(jnp.float32)
        for k in range(3):
            total = total + got[(k,) + where].astype(jnp.float32)
        return total

    for g in range(2):
        for h in range(2):
            for k in (1, 2, 3):
                step1(g, h, k).wait_recv()
            own, got, into = ((sa, ra, ta), (sb, rb, tb))[h]
            here = y if h == 0 else x

            @pl.loop(0, 4)
            def _(other):
                @pl.loop(0, 9)
                def _(tap):
                    into[g, other, tap] = summed(own.at[g, here], got.at[g], (other, tap)).astype(jnp.bfloat16)

            for k in (2, 1, 3):
                step2(g, h, k).start()

    for g in range(2):
        for h in range(2):
            for k in (1, 2, 3):
                step2(g, h, k).wait_recv()
            own, got = ((ta, tra), (tb, trb))[h]
            here = x if h == 0 else y

            @pl.loop(0, 9)
            def _(tap):
                both = summed(own.at[g, here], got.at[g], (tap,)).astype(jnp.bfloat16)
                for zz in range(2):
                    u[g, h * 2 + zz, tap] = both[zz]

        for k in (2, 1, 3):
            step3(g, k).start()

    for g in range(2):
        for k in (1, 2, 3):
            step3(g, k).wait_recv()

        @pl.loop(0, 9)
        def _(tap):
            v[g, tap] = summed(u.at[g, z], ur.at[g], (tap,))

        step4(g).start()

    for g in range(2):
        step4(g).wait_recv()

        @pl.loop(0, 9)
        def _(tap):
            fin[g, x, tap] = v[g, tap] + vr[g, tap]

        for k in (2, 1, 3):
            step5(g, k).start()

    for g in range(2):
        for k in (1, 2, 3):
            step5(g, k).wait_recv()

        @pl.loop(0, 9)
        def _(tap):
            for xx in range(4):
                outs[g][tap, :, xx * 128 : (xx + 1) * 128] = fin[g, xx, tap]

    for g in range(2):
        step0(g).wait_send()
        step4(g).wait_send()
        for k in (1, 2, 3):
            for h in range(2):
                step1(g, h, k).wait_send()
                step2(g, h, k).wait_send()
            step3(g, k).wait_send()
            step5(g, k).wait_send()


def reduce_gradients(first, second):
    bf, f32 = jnp.bfloat16, jnp.float32
    shape = (9, 16, 2, 16, 512)
    dma = pltpu.SemaphoreType.DMA
    pair = [pltpu.VMEM((2, 4, 4, 9, 2, 16, 128), bf), pltpu.VMEM((2, 3, 4, 9, 2, 16, 128), bf)]
    quad = [pltpu.VMEM((2, 4, 9, 2, 16, 128), bf), pltpu.VMEM((2, 3, 9, 2, 16, 128), bf)]
    sems = []
    for dims in ((2,), (2, 2, 4), (2, 2, 4), (2, 4), (2,), (2, 4)):
        sems += [dma(dims), dma(dims)]
    outs = pl.pallas_call(
        reduce_kernel,
        out_shape=[jax.ShapeDtypeStruct((9, 16, 512), f32)] * 2,
        in_specs=[pl.BlockSpec(memory_space=pltpu.VMEM)] * 2,
        out_specs=[pl.BlockSpec(memory_space=pltpu.VMEM)] * 2,
        scratch_shapes=[pltpu.VMEM((2, 9, 16, 16, 512), bf)]
        + pair
        + pair
        + quad
        + quad
        + [
            pltpu.VMEM((2, 4, 9, 16, 128), bf),
            pltpu.VMEM((2, 3, 9, 16, 128), bf),
            pltpu.VMEM((2, 9, 16, 128), f32),
            pltpu.VMEM((2, 9, 16, 128), f32),
            pltpu.VMEM((2, 4, 9, 16, 128), f32),
        ]
        + sems,
        compiler_params=pltpu.CompilerParams(collective_id=1, has_side_effects=True, vmem_limit_bytes=56 << 20),
        name="reduce_gradients",
    )(first.reshape(shape), second.reshape(shape))
    return [jnp.transpose(o, (1, 0, 2)) for o in outs]


def body(state, truth, conv_first, conv_second):
    members, rows, cols, channels = state.shape
    state_pad = padded(state)
    pre = conv(state_pad, conv_first, rows, cols)
    hidden = gelu_value(pre).astype(jnp.bfloat16)
    hidden_pad = padded(hidden)
    forecast = state.astype(jnp.float32) + conv(hidden_pad, conv_second, rows, cols)
    prognosis = forecast.astype(jnp.bfloat16)
    cells = rows * cols
    cot = score(forecast.reshape(members, cells, channels), truth.reshape(cells, channels))
    cot = cot.reshape(members, rows, cols, channels)
    second_terms = tap_terms(hidden_pad, cot, rows, cols)
    back = adjoint(padded(cot), conv_second, rows, cols)
    cot_pre = (back * gelu_slope(pre)).astype(jnp.bfloat16)
    first_terms = tap_terms(state_pad, cot_pre, rows, cols)
    first_slope, second_slope = reduce_gradients(first_terms, second_terms)
    return prognosis, first_slope, second_slope


def solution(mesh):
    in_specs = (P("member", "rows", None, None), P("rows", None, None), P(), P())
    out_specs = (P("member", "rows", None, None), P("rows", None, None), P("rows", None, None))
    return jax.shard_map(body, mesh=mesh, in_specs=in_specs, out_specs=out_specs, check_vma=False)
```

time: 736 us -> 182 us (0.25)
  waiting for transfers between devices: 594 us -> 11.8 us
  Pallas kernels: 0 us -> 115 us
  other arithmetic: 36.4 us -> 2.55 us
  matrix products: 39.7 us -> 20.6 us
  local copies, waits for them, and re-layouts: 26.6 us -> 12.5 us
  between operations: 14.4 us -> 1.37 us
    reduce_scatter x2 -> x0, waiting for transfers between devices: 285 us -> none  [stencil_derivative(): lax.psum_scatter(tap_terms(padded, flat_cot, meridian_extent, longitude_l...]
    all_gather x1 -> x0, waiting for transfers between devices: 177 us -> none  [body(): lax.all_gather(model_output_field, 'member', axis=0, tiled=True)]
    pallas_call x0 -> x2, Pallas kernels: none -> 115 us  [the longest x1 75.5 us: reduce_gradients(): pl.pallas_call(reduce_kernel, out_shape=[jax.ShapeDtypeStruct((9, 16, 512...]
    psum x1 -> x0, waiting for transfers between devices: 114 us -> none  [stencil_derivative(): return lax.psum(own_share, 'member')]
    add x16 -> x0, other arithmetic: 30 us -> none  [step(): return (running + spread / smooth_abs, None)]
    dot_general x45, matrix products: 39.7 us -> 20.6 us  [the longest x18 8.38 us: tap_terms(): lax.dot_general(tap_view(pad, tap, rows, cols), flat, (((0,), (0,)), ((),...]
    sub x16 -> x0, local copies, waits for them, and re-layouts: 17.3 us -> none  [step(): spread = local - other[None]]
  transfers between devices with their start and end apart: 10 -> 6, of which waited for: 7 -> 3; matrix products, arithmetic and copies ran while one was open for 3% -> 1% of each run, Pallas kernels for 0% -> 0%
where the time goes in v1:
time: 182 us; the launch traced here: 180 us
  Pallas kernels  115 us (63%)
  matrix products  20.6 us (11%)
  starting transfers between devices  16.3 us (9%)
  local copies, waits for them, and re-layouts  12.5 us (7%)
  waiting for transfers between devices  11.8 us (6%)
  other arithmetic  2.55 us (1%)
    pallas_call x1, Pallas kernels, reduce_gradients(): pl.pallas_call(reduce_kernel, out_shape=[jax.ShapeDtypeStruct((9, 16, 512...  75.5 us
    pallas_call x1, Pallas kernels, score(): pl.pallas_call(score_kernel, out_shape=jax.ShapeDtypeStruct(forecast.shap...  39.4 us
    ppermute x3, waiting for transfers between devices, padded(): high = lax.ppermute(field[:, :1], 'rows', backward)  11.8 us
    unnamed x36, local copies, waits for them, and re-layouts  9.87 us
    ppermute x3, starting transfers between devices, padded(): low = lax.ppermute(field[:, -1:], 'rows', forward)  9.04 us
    dot_general x18, matrix products, tap_terms(): lax.dot_general(tap_view(pad, tap, rows, cols), flat, (((0,), (0,)), ((),...  8.38 us
    dot_general x18, matrix products, conv(): jnp.dot(tap_view(pad, tap, rows, cols), kernel[:, tap, :], preferred_elem...  7.99 us
    ppermute x3, starting transfers between devices, padded(): high = lax.ppermute(field[:, :1], 'rows', backward)  7.27 us
  transfers between devices with their start and end apart: 6, of which 3 were waited for; matrix products, arithmetic and copies ran while one was open for 1% of the time, Pallas kernels for 0%

profile of v1, /device:TPU:1, one launch (start us, length us, event | category | flops | bytes accessed | tf_op | source)
XLA Modules:
  0.0 180.0 jit_solution(7182847849912679119)
XLA Ops:
  0.7 1.1 fusion.96
  1.8 5.1 %collective-permute-start = (bf16[2,1,64,512]{3,2,1,0:T(8,128)(2,1)S(1)}, bf16[2,1,64,512]{3,2,1,0:T(8,128)(2,1)S(1)}, u32[]{:S(2)}, u32[]{:S(2)}) collective-permute-start(bf16[2,1,64,512]{3,2,1,0:T(8,128)(2,1)S(1)} %get-tuple-element.37), channel_id=1, source_target_pairs={{0,1},{1,2},{2,3},{3,4},{4,5},{5,6},{6,7},{7,8},{8,9},{9,10},{10,1... | collective-permute-start | bytes 393224 | tf_op jit(solution)/shard_map/ppermute | solution.py:28
  6.9 1.9 %collective-permute-start.1 = (bf16[2,1,64,512]{3,2,1,0:T(8,128)(2,1)S(1)}, bf16[2,1,64,512]{3,2,1,0:T(8,128)(2,1)S(1)}, u32[]{:S(2)}, u32[]{:S(2)}) collective-permute-start(bf16[2,1,64,512]{3,2,1,0:T(8,128)(2,1)S(1)} %get-tuple-element.38), channel_id=1, source_target_pairs={{1,0},{2,1},{3,2},{4,3},{5,4},{6,5},{7,6},{8,7},{9,8},{10,9},{11,1... | collective-permute-start | bytes 393224 | tf_op jit(solution)/shard_map/ppermute | solution.py:29
  8.8 1.1 constant_dynamic-update-slice_fusion.3
  10.0 3.3 %collective-permute-done.1 = bf16[2,1,64,512]{3,2,1,0:T(8,128)(2,1)S(1)} collective-permute-done((bf16[2,1,64,512]{3,2,1,0:T(8,128)(2,1)S(1)}, bf16[2,1,64,512]{3,2,1,0:T(8,128)(2,1)S(1)}, u32[]{:S(2)}, u32[]{:S(2)}) %collective-permute-start.1) | collective-permute-done | bytes 131104 | tf_op jit(solution)/shard_map/ppermute | solution.py:29
  16.6 0.4 convolution_add_fusion.17
  18.0 0.6 multiply_convert_fusion
  18.8 2.1 %collective-permute-start.2 = (bf16[2,1,64,512]{3,2,1,0:T(8,128)(2,1)S(1)}, bf16[2,1,64,512]{3,2,1,0:T(8,128)(2,1)S(1)}, u32[]{:S(2)}, u32[]{:S(2)}) collective-permute-start(bf16[2,1,64,512]{3,2,1,0:T(8,128)(2,1)S(1)} %get-tuple-element.33), channel_id=1, source_target_pairs={{0,1},{1,2},{2,3},{3,4},{4,5},{5,6},{6,7},{7,8},{8,9},{9,10},{10,1... | collective-permute-start | bytes 393224 | tf_op jit(solution)/shard_map/ppermute | solution.py:28
  20.9 2.7 %collective-permute-start.3 = (bf16[2,1,64,512]{3,2,1,0:T(8,128)(2,1)S(1)}, bf16[2,1,64,512]{3,2,1,0:T(8,128)(2,1)S(1)}, u32[]{:S(2)}, u32[]{:S(2)}) collective-permute-start(bf16[2,1,64,512]{3,2,1,0:T(8,128)(2,1)S(1)} %get-tuple-element.34), channel_id=1, source_target_pairs={{1,0},{2,1},{3,2},{4,3},{5,4},{6,5},{7,6},{8,7},{9,8},{10,9},{11,1... | collective-permute-start | bytes 393224 | tf_op jit(solution)/shard_map/ppermute | solution.py:29
  23.6 5.3 %collective-permute-done.3 = bf16[2,1,64,512]{3,2,1,0:T(8,128)(2,1)S(1)} collective-permute-done((bf16[2,1,64,512]{3,2,1,0:T(8,128)(2,1)S(1)}, bf16[2,1,64,512]{3,2,1,0:T(8,128)(2,1)S(1)}, u32[]{:S(2)}, u32[]{:S(2)}) %collective-permute-start.3) | collective-permute-done | bytes 131104 | tf_op jit(solution)/shard_map/ppermute | solution.py:29
  29.1 0.4 fusion.92
  33.7 1.0 fusion.90
  34.7 39.4 %score.1 = bf16[2,256,512]{2,1,0:T(8,128)(2,1)S(1)} custom-call(f32[2,256,512]{2,1,0:T(8,128)S(1)} %bitcast.252, bf16[256,512]{1,0:T(8,128)(2,1)S(1)} %bitcast.253), custom_call_target="tpu_custom_call" | custom-call | tf_op jit(solution)/shard_map/score/pallas_call | solution.py:154
  74.1 0.5 convolution_convert_fusion
  74.6 0.5 convolution_convert_fusion.1
  75.1 0.5 convolution_convert_fusion.2
  75.5 0.5 convolution_convert_fusion.3
  76.0 0.5 convolution_convert_fusion.4
  76.5 0.5 convolution_convert_fusion.5
  76.9 0.5 convolution_convert_fusion.6
  77.4 0.5 convolution_convert_fusion.7
  77.9 0.5 convolution_convert_fusion.8
  78.4 1.9 %collective-permute-start.4 = (bf16[2,1,64,512]{3,2,1,0:T(8,128)(2,1)S(1)}, bf16[2,1,64,512]{3,2,1,0:T(8,128)(2,1)S(1)}, u32[]{:S(2)}, u32[]{:S(2)}) collective-permute-start(bf16[2,1,64,512]{3,2,1,0:T(8,128)(2,1)S(1)} %get-tuple-element.29), channel_id=1, source_target_pairs={{0,1},{1,2},{2,3},{3,4},{4,5},{5,6},{6,7},{7,8},{8,9},{9,10},{10,1... | collective-permute-start | bytes 393224 | tf_op jit(solution)/shard_map/ppermute | solution.py:28
  80.3 2.6 %collective-permute-start.5 = (bf16[2,1,64,512]{3,2,1,0:T(8,128)(2,1)S(1)}, bf16[2,1,64,512]{3,2,1,0:T(8,128)(2,1)S(1)}, u32[]{:S(2)}, u32[]{:S(2)}) collective-permute-start(bf16[2,1,64,512]{3,2,1,0:T(8,128)(2,1)S(1)} %get-tuple-element.30), channel_id=1, source_target_pairs={{1,0},{2,1},{3,2},{4,3},{5,4},{6,5},{7,6},{8,7},{9,8},{10,9},{11,1... | collective-permute-start | bytes 393224 | tf_op jit(solution)/shard_map/ppermute | solution.py:29
  83.3 3.2 %collective-permute-done.5 = bf16[2,1,64,512]{3,2,1,0:T(8,128)(2,1)S(1)} collective-permute-done((bf16[2,1,64,512]{3,2,1,0:T(8,128)(2,1)S(1)}, bf16[2,1,64,512]{3,2,1,0:T(8,128)(2,1)S(1)}, u32[]{:S(2)}, u32[]{:S(2)}) %collective-permute-start.5) | collective-permute-done | bytes 131104 | tf_op jit(solution)/shard_map/ppermute | solution.py:29
  87.2 0.5 fusion.42
  87.8 0.5 convolution_add_fusion.6
  88.3 0.5 convolution_add_fusion.5
  88.8 0.5 convolution_add_fusion.4
  89.2 0.5 convolution_add_fusion.3
  89.7 0.5 fusion.24
  90.2 0.5 convolution_add_fusion.2
  90.7 0.5 convolution_add_fusion.1
  91.1 0.5 fusion.1
  92.1 0.5 fusion.12
  92.5 0.5 fusion.11
  93.0 0.5 fusion.10
  93.5 0.5 fusion.9
  94.0 0.5 fusion.8
  94.4 0.5 fusion.7
  94.9 0.5 fusion.6
  95.4 0.5 fusion.5
  95.9 0.5 fusion.4
  96.8 2.2 %copy-done.3 = bf16[9,16,2,16,512]{4,3,2,1,0:T(8,128)(2,1)} copy-done((bf16[9,16,2,16,512]{4,3,2,1,0:T(8,128)(2,1)}, bf16[9,16,2,16,512]{4,3,2,1,0:T(8,128)(2,1)S(1)}, u32[]{:S(2)}) %copy-start.3) | copy-done | bytes 4718616
  98.9 2.2 %copy-done.2 = bf16[9,16,2,16,512]{4,3,2,1,0:T(8,128)(2,1)} copy-done((bf16[9,16,2,16,512]{4,3,2,1,0:T(8,128)(2,1)}, bf16[9,16,2,16,512]{4,3,2,1,0:T(8,128)(2,1)S(1)}, u32[]{:S(2)}) %copy-start.2) | copy-done | bytes 4718616
  101.1 75.5 %reduce_gradients.1 = (f32[9,16,512]{2,1,0:T(8,128)}, f32[9,16,512]{2,1,0:T(8,128)}) custom-call(bf16[9,16,2,16,512]{4,3,2,1,0:T(8,128)(2,1)} %copy-done.3, bf16[9,16,2,16,512]{4,3,2,1,0:T(8,128)(2,1)} %copy-done.2), custom_call_target="tpu_custom_call" | custom-call | tf_op jit(solution)/shard_map/reduce_gradients/pallas_call | solution.py:342
  176.7 1.7 copy.36
  178.3 1.7 copy.37
  (67 shorter events, 10.5 us)
Async XLA Ops:
  0.6 12.7 %copy-start.1 = (bf16[2,4,64,512]{3,2,1,0:T(8,128)(2,1)S(1)}, bf16[2,4,64,512]{3,2,1,0:T(8,128)(2,1)}, u32[]{:S(2)}) copy-start(bf16[2,4,64,512]{3,2,1,0:T(8,128)(2,1)} %param.4) | copy-start | bytes 1572868
  0.6 13.4 %slice-start.2 = ((s8[4718592]{0:T(1024)(128)(4,1)}), s8[4194304]{0:T(1024)(128)(4,1)S(1)}, s32[]{:S(2)}) async-start(s8[4718592]{0:T(1024)(128)(4,1)} %bitcast.259), calls=%async_computation.2 | async-start | bytes 8388608
  1.8 7.0 %collective-permute-start = (bf16[2,1,64,512]{3,2,1,0:T(8,128)(2,1)S(1)}, bf16[2,1,64,512]{3,2,1,0:T(8,128)(2,1)S(1)}, u32[]{:S(2)}, u32[]{:S(2)}) collective-permute-start(bf16[2,1,64,512]{3,2,1,0:T(8,128)(2,1)S(1)} %get-tuple-element.37), channel_id=1, source_target_pairs={{0,1},{1,2},{2,3},{3,4},{4,5},{5,6},{6,7},{7,8},{8,9},{9,10},{10,1... | collective-permute-start | bytes 393224 | tf_op jit(solution)/shard_map/ppermute | solution.py:28
  6.9 6.4 %collective-permute-start.1 = (bf16[2,1,64,512]{3,2,1,0:T(8,128)(2,1)S(1)}, bf16[2,1,64,512]{3,2,1,0:T(8,128)(2,1)S(1)}, u32[]{:S(2)}, u32[]{:S(2)}) collective-permute-start(bf16[2,1,64,512]{3,2,1,0:T(8,128)(2,1)S(1)} %get-tuple-element.38), channel_id=1, source_target_pairs={{1,0},{2,1},{3,2},{4,3},{5,4},{6,5},{7,6},{8,7},{9,8},{10,9},{11,1... | collective-permute-start | bytes 393224 | tf_op jit(solution)/shard_map/ppermute | solution.py:29
  13.4 1.0 slice-start.3
  17.9 11.6 %slice-start = ((s8[4718592]{0:T(1024)(128)(4,1)}), s8[4194304]{0:T(1024)(128)(4,1)S(1)}, s32[]{:S(2)}) async-start(s8[4718592]{0:T(1024)(128)(4,1)} %bitcast.254), calls=%async_computation | async-start | bytes 8388608
  18.8 4.8 %collective-permute-start.2 = (bf16[2,1,64,512]{3,2,1,0:T(8,128)(2,1)S(1)}, bf16[2,1,64,512]{3,2,1,0:T(8,128)(2,1)S(1)}, u32[]{:S(2)}, u32[]{:S(2)}) collective-permute-start(bf16[2,1,64,512]{3,2,1,0:T(8,128)(2,1)S(1)} %get-tuple-element.33), channel_id=1, source_target_pairs={{0,1},{1,2},{2,3},{3,4},{4,5},{5,6},{6,7},{7,8},{8,9},{9,10},{10,1... | collective-permute-start | bytes 393224 | tf_op jit(solution)/shard_map/ppermute | solution.py:28
  20.8 8.7 %slice-start.1 = ((s8[4718592]{0:T(1024)(128)(4,1)}), s8[524288]{0:T(1024)(128)(4,1)S(1)}, s32[]{:S(2)}) async-start(s8[4718592]{0:T(1024)(128)(4,1)} %bitcast.254), calls=%async_computation.1 | async-start | bytes 1048576
  20.9 8.0 %collective-permute-start.3 = (bf16[2,1,64,512]{3,2,1,0:T(8,128)(2,1)S(1)}, bf16[2,1,64,512]{3,2,1,0:T(8,128)(2,1)S(1)}, u32[]{:S(2)}, u32[]{:S(2)}) collective-permute-start(bf16[2,1,64,512]{3,2,1,0:T(8,128)(2,1)S(1)} %get-tuple-element.34), channel_id=1, source_target_pairs={{1,0},{2,1},{3,2},{4,3},{5,4},{6,5},{7,6},{8,7},{9,8},{10,9},{11,1... | collective-permute-start | bytes 393224 | tf_op jit(solution)/shard_map/ppermute | solution.py:29
  32.8 1.9 %copy-start = (bf16[4,64,512]{2,1,0:T(8,128)(2,1)S(1)}, bf16[4,64,512]{2,1,0:T(8,128)(2,1)}, u32[]{:S(2)}) copy-start(bf16[4,64,512]{2,1,0:T(8,128)(2,1)} %param.5) | copy-start | bytes 786436
  78.4 5.0 %collective-permute-start.4 = (bf16[2,1,64,512]{3,2,1,0:T(8,128)(2,1)S(1)}, bf16[2,1,64,512]{3,2,1,0:T(8,128)(2,1)S(1)}, u32[]{:S(2)}, u32[]{:S(2)}) collective-permute-start(bf16[2,1,64,512]{3,2,1,0:T(8,128)(2,1)S(1)} %get-tuple-element.29), channel_id=1, source_target_pairs={{0,1},{1,2},{2,3},{3,4},{4,5},{5,6},{6,7},{7,8},{8,9},{9,10},{10,1... | collective-permute-start | bytes 393224 | tf_op jit(solution)/shard_map/ppermute | solution.py:28
  80.3 6.3 %collective-permute-start.5 = (bf16[2,1,64,512]{3,2,1,0:T(8,128)(2,1)S(1)}, bf16[2,1,64,512]{3,2,1,0:T(8,128)(2,1)S(1)}, u32[]{:S(2)}, u32[]{:S(2)}) collective-permute-start(bf16[2,1,64,512]{3,2,1,0:T(8,128)(2,1)S(1)} %get-tuple-element.30), channel_id=1, source_target_pairs={{1,0},{2,1},{3,2},{4,3},{5,4},{6,5},{7,6},{8,7},{9,8},{10,9},{11,1... | collective-permute-start | bytes 393224 | tf_op jit(solution)/shard_map/ppermute | solution.py:29
  96.8 2.2 %copy-start.3 = (bf16[9,16,2,16,512]{4,3,2,1,0:T(8,128)(2,1)}, bf16[9,16,2,16,512]{4,3,2,1,0:T(8,128)(2,1)S(1)}, u32[]{:S(2)}) copy-start(bf16[9,16,2,16,512]{4,3,2,1,0:T(8,128)(2,1)S(1)} %get-tuple-element.41.ga) | copy-start | bytes 14155780
  98.9 2.2 %copy-start.2 = (bf16[9,16,2,16,512]{4,3,2,1,0:T(8,128)(2,1)}, bf16[9,16,2,16,512]{4,3,2,1,0:T(8,128)(2,1)S(1)}, u32[]{:S(2)}) copy-start(bf16[9,16,2,16,512]{4,3,2,1,0:T(8,128)(2,1)S(1)} %get-tuple-element.42.gb) | copy-start | bytes 14155780

commit v2 on v1

--- a/solution.py
+++ b/solution.py
@@ -42,28 +42,9 @@
     return total.reshape(pad.shape[0], rows, cols, kernel.shape[2])
 
 
-def adjoint(pad, kernel, rows, cols):
-    total = 0.0
-    for tap in range(9):
-        total = total + lax.dot_general(
-            tap_view(pad, 8 - tap, rows, cols),
-            kernel[:, tap, :],
-            (((1,), (1,)), ((), ())),
-            preferred_element_type=jnp.float32,
-        )
-    return total.reshape(pad.shape[0], rows, cols, kernel.shape[0])
-
-
-def tap_terms(pad, cot, rows, cols):
-    flat = cot.reshape(-1, cot.shape[3])
-    terms = []
-    for tap in range(9):
-        terms.append(
-            lax.dot_general(
-                tap_view(pad, tap, rows, cols), flat, (((0,), (0,)), ((), ())), preferred_element_type=jnp.float32
-            ).astype(jnp.bfloat16)
-        )
-    return jnp.stack(terms, axis=0)
+def column_shifts(pad, cols):
+    ordered = jnp.transpose(pad, (1, 0, 2, 3))
+    return jnp.stack([ordered[:, :, b : b + cols].reshape(-1, pad.shape[3]) for b in range(3)], axis=0)
 
 
 SUB = 2
@@ -166,24 +147,32 @@
     )(forecast, truth)
 
 
-def reduce_kernel(ga, gb, outa, outb, cr, sa, ra, sb, rb, ta, tra, tb, trb, u, ur, v, vr, fin, *sems):
-    s0, r0, s1, r1, s2, r2, s3, r3, s4, r4, s5, r5 = sems
+def backward_kernel(cot_ref, w_hbm, hs_hbm, xs_hbm, slope_hbm, outa, outb, *scratch):
+    (w, hs, xs, hsib, xsib, slope, cs, cp, csib, halo, ct, sa, ra, sb, rb, ta, tra, tb, trb) = scratch[:19]
+    (um, uz, ur, v, vr, fin) = scratch[19:25]
+    (local, sibs, sibr, hsend, hrecv, s1, r1, s2, r2, s3, r3, s4, r4, s5, r5) = scratch[25:]
+    bf, f32 = jnp.bfloat16, jnp.float32
     member, rows = lax.axis_index("member"), lax.axis_index("rows")
     x, zh = member // 2, lax.rem(member, 2)
     y, z, c = rows // 8, lax.rem(rows // 2, 4), lax.rem(rows, 2)
-    grads, outs = (ga, gb), (outa, outb)
+    outs = (outa, outb)
 
     def at(px, pzh, py, pz, pc):
         return {"member": px * 2 + pzh, "rows": (py * 4 + pz) * 2 + pc}
 
     sibling = at(x, zh, y, z, 1 - c)
     far = at(x, 1 - zh, y, z, c)
+    up = {"member": member, "rows": lax.rem(rows + 1, 32)}
+    down = {"member": member, "rows": lax.rem(rows + 31, 32)}
 
     def along_y(k):
         return at(x, zh, lax.rem(y + k, 4), z, c)
 
     def along_x(k):
         return at(lax.rem(x + k, 4), zh, y, z, c)
+
+    def cross_x(k):
+        return at(lax.rem(x + k, 4), zh, y, z, 1 - c)
 
     def along_z(k):
         return at(x, zh, y, lax.rem(z + k, 4), c)
@@ -193,20 +182,59 @@
             src_ref=src, dst_ref=dst, send_sem=ssem, recv_sem=rsem, device_id=to, device_id_type=MESH
         )
 
+    load_hs = pltpu.make_async_copy(hs_hbm, hs, local.at[0])
+    load_w = pltpu.make_async_copy(w_hbm, w, local.at[1])
+    load_slope = pltpu.make_async_copy(slope_hbm, slope, local.at[2])
+    load_xs = pltpu.make_async_copy(xs_hbm, xs, local.at[3])
+    load_hs.start()
+    load_w.start()
+    load_slope.start()
+    load_xs.start()
+
     barrier = pltpu.get_barrier_semaphore()
-    peers = [sibling, far] + [a(k) for a in (along_y, along_x, along_z) for k in (1, 2, 3)]
+    peers = [sibling, far, up, down]
+    peers += [a(k) for a in (along_y, along_x, cross_x, along_z) for k in (1, 2, 3)]
     for p in peers:
         pl.semaphore_signal(barrier, inc=1, device_id=p, device_id_type=MESH)
     pl.semaphore_wait(barrier, len(peers))
 
-    def step0(g):
-        return send(grads[g].at[:, :, 1 - c], cr.at[g], s0.at[g], r0.at[g], sibling)
-
-    def step1(g, h, k):
+    mine = pl.multiple_of(c * 256, 256)
+    theirs = pl.multiple_of((1 - c) * 256, 256)
+    to_up = send(cot_ref.at[pl.ds(384, 128)], halo.at[0], hsend.at[0], hrecv.at[0], up)
+    to_down = send(cot_ref.at[pl.ds(0, 128)], halo.at[1], hsend.at[1], hrecv.at[1], down)
+    cot_sib = send(cot_ref.at[:, pl.ds(theirs, 256)], csib.at[0], sibs.at[0], sibr.at[0], sibling)
+    pre_sib = send(cp.at[:, pl.ds(theirs, 256)], csib.at[1], sibs.at[1], sibr.at[1], sibling)
+    hs_sib = send(hs, hsib, sibs.at[2], sibr.at[2], sibling)
+    xs_sib = send(xs, xsib, sibs.at[3], sibr.at[3], sibling)
+    cot_sib.start()
+    to_up.start()
+    to_down.start()
+    load_hs.wait()
+    hs_sib.start()
+
+    def shifted(block, place):
+        wide = block.astype(f32)
+        col = lax.broadcasted_iota(jnp.int32, wide.shape, 0)
+        cs[0, pl.ds(place, 64)] = jnp.where(col == 0, 0.0, pltpu.roll(wide, 1, 0)).astype(bf)
+        cs[1, pl.ds(place, 64)] = block
+        cs[2, pl.ds(place, 64)] = jnp.where(col == 63, 0.0, pltpu.roll(wide, 63, 0)).astype(bf)
+
+    @pl.loop(0, 8)
+    def _(i):
+        shifted(cot_ref[pl.ds(pl.multiple_of(i * 64, 64), 64)], pl.multiple_of(128 + i * 64, 64))
+
+    def turned(value):
+        return jnp.transpose(value.astype(f32), (1, 0)).astype(bf)
+
+    def step1(g, grp, h, k):
         s, r = (sa, ra) if h == 0 else (sb, rb)
         to = lax.rem((y if h == 0 else x) + k, 4)
         return send(
-            s.at[g, to], r.at[g, k - 1], s1.at[g, h, k], r1.at[g, h, k], along_y(k) if h == 0 else along_x(k)
+            s.at[g, to, pl.ds(grp * 3, 3)],
+            r.at[g, k - 1, pl.ds(grp * 3, 3)],
+            s1.at[g, grp * 2 + h, k],
+            r1.at[g, grp * 2 + h, k],
+            along_y(k) if h == 0 else along_x(k),
         )
 
     def step2(g, h, k):
@@ -218,148 +246,198 @@
 
     def step3(g, k):
         to = lax.rem(z + k, 4)
-        return send(u.at[g, to], ur.at[g, k - 1], s3.at[g, k], r3.at[g, k], along_z(k))
+        return send(uz.at[g, to], ur.at[g, k - 1], s3.at[g, k], r3.at[g, k], along_z(k))
 
     def step4(g):
         return send(v.at[g], vr.at[g], s4.at[g], r4.at[g], far)
 
-    def step5(g, k):
-        return send(fin.at[g, x], fin.at[g, x], s5.at[g, k], r5.at[g, k], along_x(k))
-
-    for g in range(2):
-        step0(g).start()
-
-    for g in range(2):
-        step0(g).wait_recv()
-
-        @pl.loop(0, 9)
-        def _(tap):
-            @pl.loop(0, 4)
-            def _(yy):
-                for zz in range(4):
-                    block = grads[g][tap, yy * 4 + zz, c].astype(jnp.float32) + cr[g, tap, yy * 4 + zz].astype(
-                        jnp.float32
-                    )
-                    block = block.astype(jnp.bfloat16)
-                    for xx in range(4):
-                        piece = block[:, xx * 128 : (xx + 1) * 128]
-                        if zz < 2:
-                            sa[g, yy, xx, tap, zz] = piece
-                        else:
-                            sb[g, xx, yy, tap, zz - 2] = piece
-
-        for k in (2, 1, 3):
-            step1(g, 0, k).start()
-            step1(g, 1, k).start()
+    spot = c * 4 + x
+
+    def step5(g, k, cross):
+        pc = (1 - c) if cross else c
+        to = (cross_x(k) if k else sibling) if cross else along_x(k)
+        i = k + 4 * cross
+        return send(
+            um.at[g, :, pl.ds(pl.multiple_of(pc * 16, 16), 16)],
+            fin.at[g, spot],
+            s5.at[g, i],
+            r5.at[g, i],
+            to,
+        )
+
+    every5 = [(k, 0) for k in (2, 1, 3)] + [(k, 1) for k in (2, 1, 3, 0)]
+
+    def weight_gradient(g, own, sib):
+        for grp in range(3):
+
+            @pl.loop(0, 3)
+            def _(b):
+                total = jnp.dot(ct[0], own[b, grp * 128 : grp * 128 + 512], preferred_element_type=f32)
+                total = total + jnp.dot(ct[1], sib[b, grp * 128 : grp * 128 + 512], preferred_element_type=f32)
+                total = total.astype(bf)
+                for xx in range(4):
+                    for yy in range(4):
+                        for h in range(2):
+                            top = xx * 64 + h * 32
+                            piece = total[top : top + 32, yy * 128 : yy * 128 + 128]
+                            if h == 0:
+                                sa[g, yy, grp * 3 + b, xx] = piece
+                            else:
+                                sb[g, xx, grp * 3 + b, yy] = piece
+
+            for k in (2, 1, 3):
+                step1(g, grp, 0, k).start()
+                step1(g, grp, 1, k).start()
+
+    ct[0] = turned(cot_ref[:, pl.ds(mine, 256)])
+    cot_sib.wait_recv()
+    ct[1] = turned(csib[0])
+    hs_sib.wait_recv()
+    weight_gradient(0, hs, hsib)
+
+    load_xs.wait()
+    xs_sib.start()
+    to_up.wait_recv()
+    to_down.wait_recv()
+    for i in range(2):
+        below, above = halo[0, i * 64 : i * 64 + 64], halo[1, i * 64 : i * 64 + 64]
+        shifted(jnp.where(rows == 0, jnp.zeros_like(below), below), i * 64)
+        shifted(jnp.where(rows == 31, jnp.zeros_like(above), above), 640 + i * 64)
+    load_w.wait()
+    load_slope.wait()
+
+    for half in range(2):
+        lanes = pl.ds(half * 256, 256)
+        total = None
+        for tap in range(9):
+            view = cs[2 - tap % 3, pl.ds((2 - tap // 3) * 128, 512)]
+            term = lax.dot_general(view, w[tap, lanes], (((1,), (1,)), ((), ())), preferred_element_type=f32)
+            total = term if total is None else total + term
+        cp[:, lanes] = (total * slope[:, lanes]).astype(bf)
+
+    pre_sib.start()
+    ct[0] = turned(cp[:, pl.ds(mine, 256)])
+    pre_sib.wait_recv()
+    ct[1] = turned(csib[1])
+    xs_sib.wait_recv()
+    weight_gradient(1, xs, xsib)
 
     def summed(own, got, where):
-        total = own[where].astype(jnp.float32)
+        total = own[where].astype(f32)
         for k in range(3):
-            total = total + got[(k,) + where].astype(jnp.float32)
+            total = total + got[(k,) + where].astype(f32)
         return total
 
+    um[...] = jnp.zeros_like(um)
     for g in range(2):
         for h in range(2):
-            for k in (1, 2, 3):
-                step1(g, h, k).wait_recv()
+            for grp in range(3):
+                for k in (1, 2, 3):
+                    step1(g, grp, h, k).wait_recv()
             own, got, into = ((sa, ra, ta), (sb, rb, tb))[h]
             here = y if h == 0 else x
 
-            @pl.loop(0, 4)
-            def _(other):
-                @pl.loop(0, 9)
-                def _(tap):
-                    into[g, other, tap] = summed(own.at[g, here], got.at[g], (other, tap)).astype(jnp.bfloat16)
+            @pl.loop(0, 9)
+            def _(tap):
+                total = summed(own.at[g, here], got.at[g], (tap,)).astype(bf)
+                for other in range(4):
+                    into[g, other, tap] = total[other]
 
             for k in (2, 1, 3):
                 step2(g, h, k).start()
 
-    for g in range(2):
         for h in range(2):
             for k in (1, 2, 3):
                 step2(g, h, k).wait_recv()
-            own, got = ((ta, tra), (tb, trb))[h]
-            here = x if h == 0 else y
-
-            @pl.loop(0, 9)
-            def _(tap):
-                both = summed(own.at[g, here], got.at[g], (tap,)).astype(jnp.bfloat16)
-                for zz in range(2):
-                    u[g, h * 2 + zz, tap] = both[zz]
-
+        for pair in range(5):
+            blocks = []
+            for tap in (2 * pair, 2 * pair + 1):
+                for h in range(2):
+                    own, got = ((ta, tra), (tb, trb))[h]
+                    here = x if h == 0 else y
+                    blocks.append(
+                        summed(own.at[g, here], got.at[g], (tap,)) if tap < 9 else jnp.zeros((32, 128), f32)
+                    )
+            flat = jnp.transpose(jnp.concatenate(blocks, axis=0), (1, 0)).astype(bf)
+            for zz in range(4):
+                uz[g, zz, pair] = flat[zz * 32 : zz * 32 + 32]
         for k in (2, 1, 3):
             step3(g, k).start()
-
-    for g in range(2):
         for k in (1, 2, 3):
             step3(g, k).wait_recv()
-
-        @pl.loop(0, 9)
-        def _(tap):
-            v[g, tap] = summed(u.at[g, z], ur.at[g], (tap,))
-
+        v[g] = summed(uz.at[g, z], ur.at[g], (slice(None),)).astype(bf)
         step4(g).start()
+        step4(g).wait_recv()
+        um[g] = v[g].astype(f32) + vr[g].astype(f32)
+        for k, cross in every5:
+            step5(g, k, cross).start()
+        fin[g, spot] = um[g, :, pl.ds(pl.multiple_of(c * 16, 16), 16)]
 
     for g in range(2):
-        step4(g).wait_recv()
-
-        @pl.loop(0, 9)
-        def _(tap):
-            fin[g, x, tap] = v[g, tap] + vr[g, tap]
-
-        for k in (2, 1, 3):
-            step5(g, k).start()
-
+        for k, cross in every5:
+            step5(g, k, cross).wait_recv()
+        for tap in range(9):
+            off = (tap % 2) * 64
+            row = [fin[g, i, tap // 2, :, off : off + 64] for i in range(8)]
+            outs[g][tap] = jnp.concatenate(row, axis=1)
+
+    to_up.wait_send()
+    to_down.wait_send()
+    for copy in (cot_sib, pre_sib, hs_sib, xs_sib):
+        copy.wait_send()
     for g in range(2):
-        for k in (1, 2, 3):
-            step5(g, k).wait_recv()
-
-        @pl.loop(0, 9)
-        def _(tap):
-            for xx in range(4):
-                outs[g][tap, :, xx * 128 : (xx + 1) * 128] = fin[g, xx, tap]
-
-    for g in range(2):
-        step0(g).wait_send()
         step4(g).wait_send()
         for k in (1, 2, 3):
             for h in range(2):
-                step1(g, h, k).wait_send()
+                for grp in range(3):
+                    step1(g, grp, h, k).wait_send()
                 step2(g, h, k).wait_send()
             step3(g, k).wait_send()
-            step5(g, k).wait_send()
-
-
-def reduce_gradients(first, second):
+        for k, cross in every5:
+            step5(g, k, cross).wait_send()
+
+
+def backward(cot, weight, hidden_shifts, state_shifts, slope):
     bf, f32 = jnp.bfloat16, jnp.float32
-    shape = (9, 16, 2, 16, 512)
     dma = pltpu.SemaphoreType.DMA
-    pair = [pltpu.VMEM((2, 4, 4, 9, 2, 16, 128), bf), pltpu.VMEM((2, 3, 4, 9, 2, 16, 128), bf)]
-    quad = [pltpu.VMEM((2, 4, 9, 2, 16, 128), bf), pltpu.VMEM((2, 3, 9, 2, 16, 128), bf)]
-    sems = []
-    for dims in ((2,), (2, 2, 4), (2, 2, 4), (2, 4), (2,), (2, 4)):
-        sems += [dma(dims), dma(dims)]
+    vmem = pltpu.VMEM
+    pair = [vmem((2, 4, 9, 4, 32, 128), bf), vmem((2, 3, 9, 4, 32, 128), bf)]
+    quad = [vmem((2, 4, 9, 32, 128), bf), vmem((2, 3, 9, 32, 128), bf)]
+    scratch = [
+        vmem((9, 512, 512), bf),
+        vmem((3, 768, 512), bf),
+        vmem((3, 768, 512), bf),
+        vmem((3, 768, 512), bf),
+        vmem((3, 768, 512), bf),
+        vmem((512, 512), f32),
+        vmem((3, 768, 512), bf),
+        vmem((512, 512), bf),
+        vmem((2, 512, 256), bf),
+        vmem((2, 128, 512), bf),
+        vmem((2, 256, 512), bf),
+    ]
+    scratch += pair + pair + quad + quad
+    scratch += [
+        vmem((2, 5, 32, 128), f32),
+        vmem((2, 4, 5, 32, 128), bf),
+        vmem((2, 3, 5, 32, 128), bf),
+        vmem((2, 5, 32, 128), bf),
+        vmem((2, 5, 32, 128), bf),
+        vmem((2, 8, 5, 16, 128), f32),
+    ]
+    scratch += [dma((4,)), dma((4,)), dma((4,)), dma((2,)), dma((2,))]
+    for dims in ((2, 6, 4), (2, 2, 4), (2, 4), (2,), (2, 8)):
+        scratch += [dma(dims), dma(dims)]
+    any_spec = pl.BlockSpec(memory_space=pl.ANY)
     outs = pl.pallas_call(
-        reduce_kernel,
+        backward_kernel,
         out_shape=[jax.ShapeDtypeStruct((9, 16, 512), f32)] * 2,
-        in_specs=[pl.BlockSpec(memory_space=pltpu.VMEM)] * 2,
+        in_specs=[pl.BlockSpec(memory_space=pltpu.VMEM)] + [any_spec] * 4,
         out_specs=[pl.BlockSpec(memory_space=pltpu.VMEM)] * 2,
-        scratch_shapes=[pltpu.VMEM((2, 9, 16, 16, 512), bf)]
-        + pair
-        + pair
-        + quad
-        + quad
-        + [
-            pltpu.VMEM((2, 4, 9, 16, 128), bf),
-            pltpu.VMEM((2, 3, 9, 16, 128), bf),
-            pltpu.VMEM((2, 9, 16, 128), f32),
-            pltpu.VMEM((2, 9, 16, 128), f32),
-            pltpu.VMEM((2, 4, 9, 16, 128), f32),
-        ]
-        + sems,
+        scratch_shapes=scratch,
         compiler_params=pltpu.CompilerParams(collective_id=1, has_side_effects=True, vmem_limit_bytes=56 << 20),
-        name="reduce_gradients",
-    )(first.reshape(shape), second.reshape(shape))
+        name="backward",
+    )(cot, weight, hidden_shifts, state_shifts, slope)
     return [jnp.transpose(o, (1, 0, 2)) for o in outs]
 
 
@@ -374,11 +452,15 @@
     cells = rows * cols
     cot = score(forecast.reshape(members, cells, channels), truth.reshape(cells, channels))
     cot = cot.reshape(members, rows, cols, channels)
-    second_terms = tap_terms(hidden_pad, cot, rows, cols)
-    back = adjoint(padded(cot), conv_second, rows, cols)
-    cot_pre = (back * gelu_slope(pre)).astype(jnp.bfloat16)
-    first_terms = tap_terms(state_pad, cot_pre, rows, cols)
-    first_slope, second_slope = reduce_gradients(first_terms, second_terms)
+    cot = jnp.transpose(cot, (1, 0, 2, 3)).reshape(-1, channels)
+    slope = jnp.transpose(gelu_slope(pre), (1, 0, 2, 3)).reshape(-1, channels)
+    second_slope, first_slope = backward(
+        cot,
+        jnp.transpose(conv_second, (1, 0, 2)),
+        column_shifts(hidden_pad, cols),
+        column_shifts(state_pad, cols),
+        slope,
+    )
     return prognosis, first_slope, second_slope
 
 

time: 182 us -> 170 us (0.934); the launches traced: 180 us -> 170 us
  Pallas kernels: 115 us -> 128 us
  matrix products: 20.6 us -> 7.92 us
  waiting for transfers between devices: 11.8 us -> 1.93 us
  other arithmetic: 2.55 us -> 6.32 us
  starting transfers between devices: 16.3 us -> 13.3 us
    pallas_call x1, Pallas kernels: 75.5 us -> 88.9 us  [backward(): pl.pallas_call(backward_kernel, out_shape=[jax.ShapeDtypeStruct((9, 16, 5...]
    dot_general x27 -> x0, matrix products: 12.6 us -> none  [the longest x18 8.38 us: tap_terms(): lax.dot_general(tap_view(pad, tap, rows, cols), flat, (((0,), (0,)), ((),...]
    ppermute x3 -> x2, waiting for transfers between devices: 11.8 us -> 0.5 us  [padded(): high = lax.ppermute(field[:, :1], 'rows', backward)]
    unnamed x36 -> x12, local copies, waits for them, and re-layouts: 9.87 us -> 6.24 us
    ppermute x3 -> x2, starting transfers between devices: 9.04 us -> 6.27 us  [padded(): low = lax.ppermute(field[:, -1:], 'rows', forward)]
    another operation x0 -> x1, other arithmetic: none -> 2.64 us  [column_shifts(): jnp.stack([ordered[:, :, b:b + cols].reshape(-1, pad.shape[3]) for b in r...]
    ppermute x3 -> x2, starting transfers between devices: 7.27 us -> 7.07 us  [padded(): high = lax.ppermute(field[:, :1], 'rows', backward)]
  transfers between devices with their start and end apart: 6 -> 4, of which waited for: 3 -> 2; matrix products, arithmetic and copies ran while one was open for 1% -> 1% of each run, Pallas kernels for 0% -> 0%
where the time goes in v2:
time: 170 us
  Pallas kernels  128 us (75%)
  starting transfers between devices  13.3 us (8%)
  local copies, waits for them, and re-layouts  11.2 us (7%)
  matrix products  7.92 us (5%)
  other arithmetic  6.32 us (4%)
  waiting for transfers between devices  1.93 us (1%)
    pallas_call x1, Pallas kernels, backward(): pl.pallas_call(backward_kernel, out_shape=[jax.ShapeDtypeStruct((9, 16, 5...  88.9 us
    pallas_call x1, Pallas kernels, score(): pl.pallas_call(score_kernel, out_shape=jax.ShapeDtypeStruct(forecast.shap...  39.3 us
    dot_general x18, matrix products, conv(): jnp.dot(tap_view(pad, tap, rows, cols), kernel[:, tap, :], preferred_elem...  7.92 us
    ppermute x2, starting transfers between devices, padded(): high = lax.ppermute(field[:, :1], 'rows', backward)  7.07 us
    ppermute x2, starting transfers between devices, padded(): low = lax.ppermute(field[:, -1:], 'rows', forward)  6.27 us
    unnamed x12, local copies, waits for them, and re-layouts  6.24 us
  transfers between devices with their start and end apart: 4, of which 2 were waited for; matrix products, arithmetic and copies ran while one was open for 1% of the time, Pallas kernels for 0%

profile of v2, /device:TPU:1, one launch (start us, length us, event | category | flops | bytes accessed | tf_op | source)
XLA Modules:
  0.0 169.9 jit_solution(9500035911105626683)
XLA Ops:
  0.6 1.0 fusion.65
  1.6 5.1 %collective-permute-start.1 = (bf16[2,1,64,512]{3,2,1,0:T(8,128)(2,1)S(1)}, bf16[2,1,64,512]{3,2,1,0:T(8,128)(2,1)S(1)}, u32[]{:S(2)}, u32[]{:S(2)}) collective-permute-start(bf16[2,1,64,512]{3,2,1,0:T(8,128)(2,1)S(1)} %get-tuple-element.36), channel_id=1, source_target_pairs={{1,0},{2,1},{3,2},{4,3},{5,4},{6,5},{7,6},{8,7},{9,8},{10,9},{11,1... | collective-permute-start | bytes 393224 | tf_op jit(solution)/shard_map/ppermute | solution.py:29
  6.8 1.9 %collective-permute-start = (bf16[2,1,64,512]{3,2,1,0:T(8,128)(2,1)S(1)}, bf16[2,1,64,512]{3,2,1,0:T(8,128)(2,1)S(1)}, u32[]{:S(2)}, u32[]{:S(2)}) collective-permute-start(bf16[2,1,64,512]{3,2,1,0:T(8,128)(2,1)S(1)} %get-tuple-element.35), channel_id=1, source_target_pairs={{0,1},{1,2},{2,3},{3,4},{4,5},{5,6},{6,7},{7,8},{8,9},{9,10},{10,1... | collective-permute-start | bytes 393224 | tf_op jit(solution)/shard_map/ppermute | solution.py:28
  8.7 0.5 collective-permute-done.1
  9.2 1.4 collective-permute-done
  10.6 1.3 fusion.12
  11.9 0.4 fusion.63
  12.4 1.9 %copy-done.2 = bf16[512,9,512]{2,0,1:T(8,128)(2,1)S(1)} copy-done((bf16[512,9,512]{2,0,1:T(8,128)(2,1)S(1)}, bf16[512,9,512]{2,0,1:T(8,128)(2,1)}, u32[]{:S(2)}) %copy-start.2) | copy-done | bytes 4718616
  14.3 0.4 fusion.24
  14.7 0.4 fusion.33
  15.2 0.1 pad_maximum_fusion.4
  15.2 0.4 convolution_add_fusion.13
  15.7 0.4 convolution_add_fusion.12
  16.1 0.4 convolution_add_fusion.11
  16.6 0.4 convolution_add_fusion.10
  17.0 0.4 convolution_add_fusion.9
  17.5 0.4 convolution_add_fusion.8
  17.9 0.4 fusion.2
  18.4 0.5 fusion.7
  18.9 1.9 %collective-permute-start.3 = (bf16[2,1,64,512]{3,2,1,0:T(8,128)(2,1)S(1)}, bf16[2,1,64,512]{3,2,1,0:T(8,128)(2,1)S(1)}, u32[]{:S(2)}, u32[]{:S(2)}) collective-permute-start(bf16[2,1,64,512]{3,2,1,0:T(8,128)(2,1)S(1)} %get-tuple-element.32), channel_id=1, source_target_pairs={{1,0},{2,1},{3,2},{4,3},{5,4},{6,5},{7,6},{8,7},{9,8},{10,9},{11,1... | collective-permute-start | bytes 393224 | tf_op jit(solution)/shard_map/ppermute | solution.py:29
  20.8 4.4 %collective-permute-start.2 = (bf16[2,1,64,512]{3,2,1,0:T(8,128)(2,1)S(1)}, bf16[2,1,64,512]{3,2,1,0:T(8,128)(2,1)S(1)}, u32[]{:S(2)}, u32[]{:S(2)}) collective-permute-start(bf16[2,1,64,512]{3,2,1,0:T(8,128)(2,1)S(1)} %get-tuple-element.31), channel_id=1, source_target_pairs={{0,1},{1,2},{2,3},{3,4},{4,5},{5,6},{6,7},{7,8},{8,9},{9,10},{10,1... | collective-permute-start | bytes 393224 | tf_op jit(solution)/shard_map/ppermute | solution.py:28
  25.1 0.3 fusion.83
  25.4 0.4 fusion.60
  25.8 0.1 copy.22
  26.0 1.1 copy.23
  27.1 0.2 select_maximum_fusion
  27.4 0.4 fusion.62
  27.8 0.7 slice-done
  28.5 0.3 slice-done.1
  28.8 0.4 fusion.13
  29.2 0.4 fusion.22
  29.7 0.1 pad_maximum_fusion.2
  29.7 0.4 convolution_add_fusion.6
  30.2 0.4 convolution_add_fusion.5
  30.6 0.4 convolution_add_fusion.4
  31.1 0.5 convolution_add_fusion.3
  31.6 0.4 convolution_add_fusion.2
  32.0 0.4 convolution_add_fusion.1
  32.5 0.4 fusion.1
  32.9 1.0 fusion.59
  34.0 39.3 %score.1 = bf16[2,256,512]{2,1,0:T(8,128)(2,1)S(1)} custom-call(f32[2,256,512]{2,1,0:T(8,128)S(1)} %bitcast.112, bf16[256,512]{1,0:T(8,128)(2,1)S(1)} %bitcast.114), custom_call_target="tpu_custom_call" | custom-call | tf_op jit(solution)/shard_map/score/pallas_call | solution.py:135
  73.3 0.8 copy.16
  74.1 0.2 fusion.84
  74.4 0.4 fusion.61
  75.0 2.6 %pad_maximum_fusion = (bf16[3,768,512]{2,1,0:T(8,128)(2,1)}, bf16[3,768,512]{2,1,0:T(8,128)(2,1)}) fusion(bf16[1,768,512]{2,1,0:T(8,128)(2,1)S(1)} %bitcast.125, bf16[1,768,512]{2,1,0:T(8,128)(2,1)S(1)} %bitcast.126, bf16[1,768,512]{2,1,0:T(8,128)(2,1)S(1)} %bitcast.127, bf16[1,768,512]{2,1,0:T(8,128)(2,1)S(1)} %bitcast.122, ...), kind=kLoop, calls=%fused_computation.2 | loop fusion | flops 4718592 | bytes 9437184 | tf_op jit(solution)/shard_map/stack | solution.py:47
  77.6 88.9 %backward.1 = (f32[9,16,512]{2,1,0:T(8,128)}, f32[9,16,512]{2,1,0:T(8,128)}) custom-call(bf16[512,512]{1,0:T(8,128)(2,1)} %bitcast.144, bf16[9,512,512]{2,1,0:T(8,128)(2,1)} %bitcast.115, bf16[3,768,512]{2,1,0:T(8,128)(2,1)} %get-tuple-element.37.hs_hbm, bf16[3,768,512]{2,1,0:T(8,128)(2,1)} %get-tuple-element.38.xs_hbm, f32[512,512]{1,0:T(8,128)} %bitcast.121), custom_call_target="tpu_custom_call" | custom-call | tf_op jit(solution)/shard_map/backward/pallas_call | solution.py:432
  166.5 1.7 copy.26
  168.2 1.7 copy.27
  (16 shorter events, 0.3 us)
Async XLA Ops:
  1.6 7.6 %collective-permute-start.1 = (bf16[2,1,64,512]{3,2,1,0:T(8,128)(2,1)S(1)}, bf16[2,1,64,512]{3,2,1,0:T(8,128)(2,1)S(1)}, u32[]{:S(2)}, u32[]{:S(2)}) collective-permute-start(bf16[2,1,64,512]{3,2,1,0:T(8,128)(2,1)S(1)} %get-tuple-element.36), channel_id=1, source_target_pairs={{1,0},{2,1},{3,2},{4,3},{5,4},{6,5},{7,6},{8,7},{9,8},{10,9},{11,1... | collective-permute-start | bytes 393224 | tf_op jit(solution)/shard_map/ppermute | solution.py:29
  6.8 3.9 %collective-permute-start = (bf16[2,1,64,512]{3,2,1,0:T(8,128)(2,1)S(1)}, bf16[2,1,64,512]{3,2,1,0:T(8,128)(2,1)S(1)}, u32[]{:S(2)}, u32[]{:S(2)}) collective-permute-start(bf16[2,1,64,512]{3,2,1,0:T(8,128)(2,1)S(1)} %get-tuple-element.35), channel_id=1, source_target_pairs={{0,1},{1,2},{2,3},{3,4},{4,5},{5,6},{6,7},{7,8},{8,9},{9,10},{10,1... | collective-permute-start | bytes 393224 | tf_op jit(solution)/shard_map/ppermute | solution.py:28
  11.9 2.3 %copy-start.2 = (bf16[512,9,512]{2,0,1:T(8,128)(2,1)S(1)}, bf16[512,9,512]{2,0,1:T(8,128)(2,1)}, u32[]{:S(2)}) copy-start(bf16[512,9,512]{2,0,1:T(8,128)(2,1)} %param.6) | copy-start | bytes 14155780
  12.4 2.8 %copy-start.1 = (bf16[2,4,64,512]{3,2,1,0:T(8,128)(2,1)S(1)}, bf16[2,4,64,512]{3,2,1,0:T(8,128)(2,1)}, u32[]{:S(2)}) copy-start(bf16[2,4,64,512]{3,2,1,0:T(8,128)(2,1)} %param.4) | copy-start | bytes 1572868
  18.9 8.2 %collective-permute-start.3 = (bf16[2,1,64,512]{3,2,1,0:T(8,128)(2,1)S(1)}, bf16[2,1,64,512]{3,2,1,0:T(8,128)(2,1)S(1)}, u32[]{:S(2)}, u32[]{:S(2)}) collective-permute-start(bf16[2,1,64,512]{3,2,1,0:T(8,128)(2,1)S(1)} %get-tuple-element.32), channel_id=1, source_target_pairs={{1,0},{2,1},{3,2},{4,3},{5,4},{6,5},{7,6},{8,7},{9,8},{10,9},{11,1... | collective-permute-start | bytes 393224 | tf_op jit(solution)/shard_map/ppermute | solution.py:29
  20.8 6.3 %collective-permute-start.2 = (bf16[2,1,64,512]{3,2,1,0:T(8,128)(2,1)S(1)}, bf16[2,1,64,512]{3,2,1,0:T(8,128)(2,1)S(1)}, u32[]{:S(2)}, u32[]{:S(2)}) collective-permute-start(bf16[2,1,64,512]{3,2,1,0:T(8,128)(2,1)S(1)} %get-tuple-element.31), channel_id=1, source_target_pairs={{0,1},{1,2},{2,3},{3,4},{4,5},{5,6},{6,7},{7,8},{8,9},{9,10},{10,1... | collective-permute-start | bytes 393224 | tf_op jit(solution)/shard_map/ppermute | solution.py:28
  25.9 2.6 %slice-start = ((s8[4718592]{0:T(1024)(128)(4,1)}), s8[4194304]{0:T(1024)(128)(4,1)S(1)}, s32[]{:S(2)}) async-start(s8[4718592]{0:T(1024)(128)(4,1)} %bitcast.116), calls=%async_computation | async-start | bytes 8388608
  27.1 1.7 slice-start.1
  32.9 1.0 copy-start

commit v3 on v2

--- a/solution.py
+++ b/solution.py
@@ -147,10 +147,13 @@
     )(forecast, truth)
 
 
+SIZES = (4, 4, 1)
+
+
 def backward_kernel(cot_ref, w_hbm, hs_hbm, xs_hbm, slope_hbm, outa, outb, *scratch):
     (w, hs, xs, hsib, xsib, slope, cs, cp, csib, halo, ct, sa, ra, sb, rb, ta, tra, tb, trb) = scratch[:19]
-    (um, uz, ur, v, vr, fin) = scratch[19:25]
-    (local, sibs, sibr, hsend, hrecv, s1, r1, s2, r2, s3, r3, s4, r4, s5, r5) = scratch[25:]
+    (um, uz, ur, fin) = scratch[19:23]
+    (local, sibs, sibr, hsend, hrecv, s1, r1, s2, r2, s3, r3, s5, r5) = scratch[23:]
     bf, f32 = jnp.bfloat16, jnp.float32
     member, rows = lax.axis_index("member"), lax.axis_index("rows")
     x, zh = member // 2, lax.rem(member, 2)
@@ -161,7 +164,6 @@
         return {"member": px * 2 + pzh, "rows": (py * 4 + pz) * 2 + pc}
 
     sibling = at(x, zh, y, z, 1 - c)
-    far = at(x, 1 - zh, y, z, c)
     up = {"member": member, "rows": lax.rem(rows + 1, 32)}
     down = {"member": member, "rows": lax.rem(rows + 31, 32)}
 
@@ -174,8 +176,11 @@
     def cross_x(k):
         return at(lax.rem(x + k, 4), zh, y, z, 1 - c)
 
+    ring = zh * 4 + z
+
     def along_z(k):
-        return at(x, zh, y, lax.rem(z + k, 4), c)
+        to = lax.rem(ring + k, 8)
+        return at(x, to // 4, y, lax.rem(to, 4), c)
 
     def send(src, dst, ssem, rsem, to):
         return pltpu.make_async_remote_copy(
@@ -192,8 +197,8 @@
     load_xs.start()
 
     barrier = pltpu.get_barrier_semaphore()
-    peers = [sibling, far, up, down]
-    peers += [a(k) for a in (along_y, along_x, cross_x, along_z) for k in (1, 2, 3)]
+    peers = [sibling, up, down] + [along_z(k) for k in range(1, 8)]
+    peers += [a(k) for a in (along_y, along_x, cross_x) for k in (1, 2, 3)]
     for p in peers:
         pl.semaphore_signal(barrier, inc=1, device_id=p, device_id_type=MESH)
     pl.semaphore_wait(barrier, len(peers))
@@ -226,30 +231,34 @@
     def turned(value):
         return jnp.transpose(value.astype(f32), (1, 0)).astype(bf)
 
-    def step1(g, grp, h, k):
+    def step1(g, part, h, k):
         s, r = (sa, ra) if h == 0 else (sb, rb)
         to = lax.rem((y if h == 0 else x) + k, 4)
+        taps = pl.ds(part * 4, SIZES[part])
         return send(
-            s.at[g, to, pl.ds(grp * 3, 3)],
-            r.at[g, k - 1, pl.ds(grp * 3, 3)],
-            s1.at[g, grp * 2 + h, k],
-            r1.at[g, grp * 2 + h, k],
+            s.at[g, to, taps],
+            r.at[g, k - 1, taps],
+            s1.at[g, part * 2 + h, k],
+            r1.at[g, part * 2 + h, k],
             along_y(k) if h == 0 else along_x(k),
         )
 
-    def step2(g, h, k):
+    def step2(g, part, h, k):
         s, r = (ta, tra) if h == 0 else (tb, trb)
         to = lax.rem((x if h == 0 else y) + k, 4)
+        taps = pl.ds(part * 4, SIZES[part])
         return send(
-            s.at[g, to], r.at[g, k - 1], s2.at[g, h, k], r2.at[g, h, k], along_x(k) if h == 0 else along_y(k)
+            s.at[g, to, taps],
+            r.at[g, k - 1, taps],
+            s2.at[g, part * 2 + h, k],
+            r2.at[g, part * 2 + h, k],
+            along_x(k) if h == 0 else along_y(k),
         )
 
-    def step3(g, k):
-        to = lax.rem(z + k, 4)
-        return send(uz.at[g, to], ur.at[g, k - 1], s3.at[g, k], r3.at[g, k], along_z(k))
-
-    def step4(g):
-        return send(v.at[g], vr.at[g], s4.at[g], r4.at[g], far)
+    def step3(g, part, k):
+        to = lax.rem(lax.rem(ring + k, 8), 4)
+        pairs = pl.ds(part * 2, (SIZES[part] + 1) // 2)
+        return send(uz.at[g, to, pairs], ur.at[g, ring, pairs], s3.at[g, part, k], r3.at[g, part, k], along_z(k))
 
     spot = c * 4 + x
 
@@ -257,70 +266,31 @@
         pc = (1 - c) if cross else c
         to = (cross_x(k) if k else sibling) if cross else along_x(k)
         i = k + 4 * cross
-        return send(
-            um.at[g, :, pl.ds(pl.multiple_of(pc * 16, 16), 16)],
-            fin.at[g, spot],
-            s5.at[g, i],
-            r5.at[g, i],
-            to,
-        )
+        return send(um.at[g, pc], fin.at[g, spot], s5.at[g, i], r5.at[g, i], to)
 
     every5 = [(k, 0) for k in (2, 1, 3)] + [(k, 1) for k in (2, 1, 3, 0)]
 
-    def weight_gradient(g, own, sib):
-        for grp in range(3):
-
-            @pl.loop(0, 3)
-            def _(b):
-                total = jnp.dot(ct[0], own[b, grp * 128 : grp * 128 + 512], preferred_element_type=f32)
-                total = total + jnp.dot(ct[1], sib[b, grp * 128 : grp * 128 + 512], preferred_element_type=f32)
-                total = total.astype(bf)
-                for xx in range(4):
-                    for yy in range(4):
-                        for h in range(2):
-                            top = xx * 64 + h * 32
-                            piece = total[top : top + 32, yy * 128 : yy * 128 + 128]
-                            if h == 0:
-                                sa[g, yy, grp * 3 + b, xx] = piece
-                            else:
-                                sb[g, xx, grp * 3 + b, yy] = piece
-
-            for k in (2, 1, 3):
-                step1(g, grp, 0, k).start()
-                step1(g, grp, 1, k).start()
-
-    ct[0] = turned(cot_ref[:, pl.ds(mine, 256)])
-    cot_sib.wait_recv()
-    ct[1] = turned(csib[0])
-    hs_sib.wait_recv()
-    weight_gradient(0, hs, hsib)
-
-    load_xs.wait()
-    xs_sib.start()
-    to_up.wait_recv()
-    to_down.wait_recv()
-    for i in range(2):
-        below, above = halo[0, i * 64 : i * 64 + 64], halo[1, i * 64 : i * 64 + 64]
-        shifted(jnp.where(rows == 0, jnp.zeros_like(below), below), i * 64)
-        shifted(jnp.where(rows == 31, jnp.zeros_like(above), above), 640 + i * 64)
-    load_w.wait()
-    load_slope.wait()
-
-    for half in range(2):
-        lanes = pl.ds(half * 256, 256)
-        total = None
-        for tap in range(9):
-            view = cs[2 - tap % 3, pl.ds((2 - tap // 3) * 128, 512)]
-            term = lax.dot_general(view, w[tap, lanes], (((1,), (1,)), ((), ())), preferred_element_type=f32)
-            total = term if total is None else total + term
-        cp[:, lanes] = (total * slope[:, lanes]).astype(bf)
-
-    pre_sib.start()
-    ct[0] = turned(cp[:, pl.ds(mine, 256)])
-    pre_sib.wait_recv()
-    ct[1] = turned(csib[1])
-    xs_sib.wait_recv()
-    weight_gradient(1, xs, xsib)
+    def form(g, part, own, sib):
+        @pl.loop(part * 4, part * 4 + SIZES[part])
+        def _(tap):
+            b = lax.rem(tap, 3)
+            view = pl.ds(pl.multiple_of((tap // 3) * 128, 128), 512)
+            total = jnp.dot(ct[0], own[b, view], preferred_element_type=f32)
+            total = total + jnp.dot(ct[1], sib[b, view], preferred_element_type=f32)
+            total = total.astype(bf)
+            for xx in range(4):
+                for yy in range(4):
+                    for h in range(2):
+                        top = xx * 64 + h * 32
+                        piece = total[top : top + 32, yy * 128 : yy * 128 + 128]
+                        if h == 0:
+                            sa[g, yy, tap, xx] = piece
+                        else:
+                            sb[g, xx, tap, yy] = piece
+
+        for k in (2, 1, 3):
+            step1(g, part, 0, k).start()
+            step1(g, part, 1, k).start()
 
     def summed(own, got, where):
         total = own[where].astype(f32)
@@ -328,28 +298,27 @@
             total = total + got[(k,) + where].astype(f32)
         return total
 
-    um[...] = jnp.zeros_like(um)
-    for g in range(2):
+    def add1(g, part):
         for h in range(2):
-            for grp in range(3):
-                for k in (1, 2, 3):
-                    step1(g, grp, h, k).wait_recv()
+            for k in (1, 2, 3):
+                step1(g, part, h, k).wait_recv()
             own, got, into = ((sa, ra, ta), (sb, rb, tb))[h]
             here = y if h == 0 else x
 
-            @pl.loop(0, 9)
+            @pl.loop(part * 4, part * 4 + SIZES[part])
             def _(tap):
                 total = summed(own.at[g, here], got.at[g], (tap,)).astype(bf)
                 for other in range(4):
                     into[g, other, tap] = total[other]
 
             for k in (2, 1, 3):
-                step2(g, h, k).start()
-
+                step2(g, part, h, k).start()
+
+    def add2(g, part):
         for h in range(2):
             for k in (1, 2, 3):
-                step2(g, h, k).wait_recv()
-        for pair in range(5):
+                step2(g, part, h, k).wait_recv()
+        for pair in range(part * 2, part * 2 + (SIZES[part] + 1) // 2):
             blocks = []
             for tap in (2 * pair, 2 * pair + 1):
                 for h in range(2):
@@ -361,38 +330,105 @@
             flat = jnp.transpose(jnp.concatenate(blocks, axis=0), (1, 0)).astype(bf)
             for zz in range(4):
                 uz[g, zz, pair] = flat[zz * 32 : zz * 32 + 32]
-        for k in (2, 1, 3):
-            step3(g, k).start()
-        for k in (1, 2, 3):
-            step3(g, k).wait_recv()
-        v[g] = summed(uz.at[g, z], ur.at[g], (slice(None),)).astype(bf)
-        step4(g).start()
-        step4(g).wait_recv()
-        um[g] = v[g].astype(f32) + vr[g].astype(f32)
+        for k in (4, 3, 5, 2, 6, 1, 7):
+            step3(g, part, k).start()
+        pairs = pl.ds(part * 2, (SIZES[part] + 1) // 2)
+        ur[g, ring, pairs] = uz[g, z, pairs]
+
+    def add3(g, part):
+        for k in range(1, 8):
+            step3(g, part, k).wait_recv()
+        pairs = slice(part * 2, part * 2 + (SIZES[part] + 1) // 2)
+        total = ur[g, 0, pairs].astype(f32)
+        for q in range(1, 8):
+            total = total + ur[g, q, pairs].astype(f32)
+        total = total.astype(bf)
+        um[g, 0, pairs] = total[:, :16]
+        um[g, 1, pairs] = total[:, 16:]
+
+    def spread(g):
         for k, cross in every5:
             step5(g, k, cross).start()
-        fin[g, spot] = um[g, :, pl.ds(pl.multiple_of(c * 16, 16), 16)]
-
-    for g in range(2):
+        fin[g, spot] = um[g, c]
+
+    def finish(g):
         for k, cross in every5:
             step5(g, k, cross).wait_recv()
         for tap in range(9):
             off = (tap % 2) * 64
-            row = [fin[g, i, tap // 2, :, off : off + 64] for i in range(8)]
+            row = [fin[g, i, tap // 2, :, off : off + 64].astype(f32) for i in range(8)]
             outs[g][tap] = jnp.concatenate(row, axis=1)
+
+    ct[0] = turned(cot_ref[:, pl.ds(mine, 256)])
+    cot_sib.wait_recv()
+    ct[1] = turned(csib[0])
+    hs_sib.wait_recv()
+    for part in range(3):
+        form(0, part, hs, hsib)
+
+    load_xs.wait()
+    xs_sib.start()
+    to_up.wait_recv()
+    to_down.wait_recv()
+    for i in range(2):
+        below, above = halo[0, i * 64 : i * 64 + 64], halo[1, i * 64 : i * 64 + 64]
+        shifted(jnp.where(rows == 0, jnp.zeros_like(below), below), i * 64)
+        shifted(jnp.where(rows == 31, jnp.zeros_like(above), above), 640 + i * 64)
+    load_w.wait()
+    load_slope.wait()
+
+    for half in range(2):
+        lanes = pl.ds(half * 256, 256)
+        total = None
+        for tap in range(9):
+            view = cs[2 - tap % 3, pl.ds((2 - tap // 3) * 128, 512)]
+            term = lax.dot_general(view, w[tap, lanes], (((1,), (1,)), ((), ())), preferred_element_type=f32)
+            total = term if total is None else total + term
+        cp[:, lanes] = (total * slope[:, lanes]).astype(bf)
+
+    pre_sib.start()
+    ct[0] = turned(cp[:, pl.ds(mine, 256)])
+    pre_sib.wait_recv()
+    ct[1] = turned(csib[1])
+    xs_sib.wait_recv()
+    add1(0, 0)
+    form(1, 0, xs, xsib)
+    add1(0, 1)
+    form(1, 1, xs, xsib)
+    add2(0, 0)
+    form(1, 2, xs, xsib)
+    add1(0, 2)
+    add2(0, 1)
+    add2(0, 2)
+    add1(1, 0)
+    add3(0, 0)
+    add3(0, 1)
+    add3(0, 2)
+    spread(0)
+    add2(1, 0)
+    add1(1, 1)
+    add1(1, 2)
+    add2(1, 1)
+    add2(1, 2)
+    finish(0)
+    add3(1, 0)
+    add3(1, 1)
+    add3(1, 2)
+    spread(1)
+    finish(1)
 
     to_up.wait_send()
     to_down.wait_send()
     for copy in (cot_sib, pre_sib, hs_sib, xs_sib):
         copy.wait_send()
     for g in range(2):
-        step4(g).wait_send()
-        for k in (1, 2, 3):
-            for h in range(2):
-                for grp in range(3):
-                    step1(g, grp, h, k).wait_send()
-                step2(g, h, k).wait_send()
-            step3(g, k).wait_send()
+        for part in range(3):
+            for k in (1, 2, 3):
+                for h in range(2):
+                    step1(g, part, h, k).wait_send()
+                    step2(g, part, h, k).wait_send()
+            for k in range(1, 8):
+                step3(g, part, k).wait_send()
         for k, cross in every5:
             step5(g, k, cross).wait_send()
 
@@ -418,15 +454,13 @@
     ]
     scratch += pair + pair + quad + quad
     scratch += [
-        vmem((2, 5, 32, 128), f32),
+        vmem((2, 2, 5, 16, 128), bf),
         vmem((2, 4, 5, 32, 128), bf),
-        vmem((2, 3, 5, 32, 128), bf),
-        vmem((2, 5, 32, 128), bf),
-        vmem((2, 5, 32, 128), bf),
-        vmem((2, 8, 5, 16, 128), f32),
+        vmem((2, 8, 5, 32, 128), bf),
+        vmem((2, 8, 5, 16, 128), bf),
     ]
     scratch += [dma((4,)), dma((4,)), dma((4,)), dma((2,)), dma((2,))]
-    for dims in ((2, 6, 4), (2, 2, 4), (2, 4), (2,), (2, 8)):
+    for dims in ((2, 6, 4), (2, 6, 4), (2, 3, 8), (2, 8)):
         scratch += [dma(dims), dma(dims)]
     any_spec = pl.BlockSpec(memory_space=pl.ANY)
     outs = pl.pallas_call(

time: 170 us -> 160 us (0.941)
  Pallas kernels: 128 us -> 118 us
    pallas_call x1, Pallas kernels: 88.9 us -> 78.8 us  [backward(): pl.pallas_call(backward_kernel, out_shape=[jax.ShapeDtypeStruct((9, 16, 5...]
where the time goes in v3:
time: 160 us
  Pallas kernels  118 us (74%)
  starting transfers between devices  13.3 us (8%)
  local copies, waits for them, and re-layouts  11.2 us (7%)
  matrix products  7.92 us (5%)
  other arithmetic  6.32 us (4%)
  waiting for transfers between devices  1.93 us (1%)
    pallas_call x1, Pallas kernels, backward(): pl.pallas_call(backward_kernel, out_shape=[jax.ShapeDtypeStruct((9, 16, 5...  78.8 us
    pallas_call x1, Pallas kernels, score(): pl.pallas_call(score_kernel, out_shape=jax.ShapeDtypeStruct(forecast.shap...  39.3 us
    dot_general x18, matrix products, conv(): jnp.dot(tap_view(pad, tap, rows, cols), kernel[:, tap, :], preferred_elem...  7.92 us
    ppermute x2, starting transfers between devices, padded(): high = lax.ppermute(field[:, :1], 'rows', backward)  7.07 us
    ppermute x2, starting transfers between devices, padded(): low = lax.ppermute(field[:, -1:], 'rows', forward)  6.27 us
    unnamed x12, local copies, waits for them, and re-layouts  6.24 us
  transfers between devices with their start and end apart: 4, of which 2 were waited for; matrix products, arithmetic and copies ran while one was open for 1% of the time, Pallas kernels for 0%

profile of v3, /device:TPU:1, one launch (start us, length us, event | category | flops | bytes accessed | tf_op | source)
XLA Modules:
  0.0 159.8 jit_solution(693610948079149173)
XLA Ops:
  0.6 1.0 fusion.65
  1.6 5.1 %collective-permute-start.1 = (bf16[2,1,64,512]{3,2,1,0:T(8,128)(2,1)S(1)}, bf16[2,1,64,512]{3,2,1,0:T(8,128)(2,1)S(1)}, u32[]{:S(2)}, u32[]{:S(2)}) collective-permute-start(bf16[2,1,64,512]{3,2,1,0:T(8,128)(2,1)S(1)} %get-tuple-element.36), channel_id=1, source_target_pairs={{1,0},{2,1},{3,2},{4,3},{5,4},{6,5},{7,6},{8,7},{9,8},{10,9},{11,1... | collective-permute-start | bytes 393224 | tf_op jit(solution)/shard_map/ppermute | solution.py:29
  6.8 1.9 %collective-permute-start = (bf16[2,1,64,512]{3,2,1,0:T(8,128)(2,1)S(1)}, bf16[2,1,64,512]{3,2,1,0:T(8,128)(2,1)S(1)}, u32[]{:S(2)}, u32[]{:S(2)}) collective-permute-start(bf16[2,1,64,512]{3,2,1,0:T(8,128)(2,1)S(1)} %get-tuple-element.35), channel_id=1, source_target_pairs={{0,1},{1,2},{2,3},{3,4},{4,5},{5,6},{6,7},{7,8},{8,9},{9,10},{10,1... | collective-permute-start | bytes 393224 | tf_op jit(solution)/shard_map/ppermute | solution.py:28
  8.7 0.5 collective-permute-done.1
  9.2 1.4 collective-permute-done
  10.6 1.3 fusion.12
  11.9 0.4 fusion.63
  12.4 1.9 %copy-done.2 = bf16[512,9,512]{2,0,1:T(8,128)(2,1)S(1)} copy-done((bf16[512,9,512]{2,0,1:T(8,128)(2,1)S(1)}, bf16[512,9,512]{2,0,1:T(8,128)(2,1)}, u32[]{:S(2)}) %copy-start.2) | copy-done | bytes 4718616
  14.3 0.4 fusion.24
  14.7 0.4 fusion.33
  15.2 0.1 pad_maximum_fusion.4
  15.2 0.4 convolution_add_fusion.13
  15.7 0.4 convolution_add_fusion.12
  16.1 0.4 convolution_add_fusion.11
  16.6 0.4 convolution_add_fusion.10
  17.0 0.4 convolution_add_fusion.9
  17.5 0.4 convolution_add_fusion.8
  17.9 0.4 fusion.2
  18.4 0.5 fusion.7
  18.9 1.9 %collective-permute-start.3 = (bf16[2,1,64,512]{3,2,1,0:T(8,128)(2,1)S(1)}, bf16[2,1,64,512]{3,2,1,0:T(8,128)(2,1)S(1)}, u32[]{:S(2)}, u32[]{:S(2)}) collective-permute-start(bf16[2,1,64,512]{3,2,1,0:T(8,128)(2,1)S(1)} %get-tuple-element.32), channel_id=1, source_target_pairs={{1,0},{2,1},{3,2},{4,3},{5,4},{6,5},{7,6},{8,7},{9,8},{10,9},{11,1... | collective-permute-start | bytes 393224 | tf_op jit(solution)/shard_map/ppermute | solution.py:29
  20.8 4.4 %collective-permute-start.2 = (bf16[2,1,64,512]{3,2,1,0:T(8,128)(2,1)S(1)}, bf16[2,1,64,512]{3,2,1,0:T(8,128)(2,1)S(1)}, u32[]{:S(2)}, u32[]{:S(2)}) collective-permute-start(bf16[2,1,64,512]{3,2,1,0:T(8,128)(2,1)S(1)} %get-tuple-element.31), channel_id=1, source_target_pairs={{0,1},{1,2},{2,3},{3,4},{4,5},{5,6},{6,7},{7,8},{8,9},{9,10},{10,1... | collective-permute-start | bytes 393224 | tf_op jit(solution)/shard_map/ppermute | solution.py:28
  25.1 0.3 fusion.83
  25.4 0.4 fusion.60
  25.8 0.1 copy.22
  26.0 1.1 copy.23
  27.1 0.2 select_maximum_fusion
  27.4 0.4 fusion.62
  27.8 0.7 slice-done
  28.5 0.3 slice-done.1
  28.8 0.4 fusion.13
  29.2 0.4 fusion.22
  29.7 0.1 pad_maximum_fusion.2
  29.7 0.4 convolution_add_fusion.6
  30.2 0.4 convolution_add_fusion.5
  30.6 0.4 convolution_add_fusion.4
  31.1 0.5 convolution_add_fusion.3
  31.6 0.4 convolution_add_fusion.2
  32.0 0.4 convolution_add_fusion.1
  32.5 0.4 fusion.1
  32.9 1.0 fusion.59
  34.0 39.3 %score.1 = bf16[2,256,512]{2,1,0:T(8,128)(2,1)S(1)} custom-call(f32[2,256,512]{2,1,0:T(8,128)S(1)} %bitcast.112, bf16[256,512]{1,0:T(8,128)(2,1)S(1)} %bitcast.114), custom_call_target="tpu_custom_call" | custom-call | tf_op jit(solution)/shard_map/score/pallas_call | solution.py:135
  73.3 0.8 copy.16
  74.1 0.2 fusion.84
  74.4 0.4 fusion.61
  75.0 2.6 %pad_maximum_fusion = (bf16[3,768,512]{2,1,0:T(8,128)(2,1)}, bf16[3,768,512]{2,1,0:T(8,128)(2,1)}) fusion(bf16[1,768,512]{2,1,0:T(8,128)(2,1)S(1)} %bitcast.125, bf16[1,768,512]{2,1,0:T(8,128)(2,1)S(1)} %bitcast.126, bf16[1,768,512]{2,1,0:T(8,128)(2,1)S(1)} %bitcast.127, bf16[1,768,512]{2,1,0:T(8,128)(2,1)S(1)} %bitcast.122, ...), kind=kLoop, calls=%fused_computation.2 | loop fusion | flops 4718592 | bytes 9437184 | tf_op jit(solution)/shard_map/stack | solution.py:47
  77.6 78.8 %backward.1 = (f32[9,16,512]{2,1,0:T(8,128)}, f32[9,16,512]{2,1,0:T(8,128)}) custom-call(bf16[512,512]{1,0:T(8,128)(2,1)} %bitcast.144, bf16[9,512,512]{2,1,0:T(8,128)(2,1)} %bitcast.115, bf16[3,768,512]{2,1,0:T(8,128)(2,1)} %get-tuple-element.37.hs_hbm, bf16[3,768,512]{2,1,0:T(8,128)(2,1)} %get-tuple-element.38.xs_hbm, f32[512,512]{1,0:T(8,128)} %bitcast.121), custom_call_target="tpu_custom_call" | custom-call | tf_op jit(solution)/shard_map/backward/pallas_call | solution.py:466
  156.4 1.7 %copy.26 = f32[16,9,512]{2,0,1:T(8,128)} copy(f32[16,9,512]{2,0,1:T(8,128)} %bitcast.146) | data formatting | bytes 589824
  158.1 1.7 %copy.27 = f32[16,9,512]{2,0,1:T(8,128)} copy(f32[16,9,512]{2,0,1:T(8,128)} %bitcast.145) | data formatting | bytes 589824
  (16 shorter events, 0.3 us)
Async XLA Ops:
  1.6 7.6 %collective-permute-start.1 = (bf16[2,1,64,512]{3,2,1,0:T(8,128)(2,1)S(1)}, bf16[2,1,64,512]{3,2,1,0:T(8,128)(2,1)S(1)}, u32[]{:S(2)}, u32[]{:S(2)}) collective-permute-start(bf16[2,1,64,512]{3,2,1,0:T(8,128)(2,1)S(1)} %get-tuple-element.36), channel_id=1, source_target_pairs={{1,0},{2,1},{3,2},{4,3},{5,4},{6,5},{7,6},{8,7},{9,8},{10,9},{11,1... | collective-permute-start | bytes 393224 | tf_op jit(solution)/shard_map/ppermute | solution.py:29
  6.8 3.9 %collective-permute-start = (bf16[2,1,64,512]{3,2,1,0:T(8,128)(2,1)S(1)}, bf16[2,1,64,512]{3,2,1,0:T(8,128)(2,1)S(1)}, u32[]{:S(2)}, u32[]{:S(2)}) collective-permute-start(bf16[2,1,64,512]{3,2,1,0:T(8,128)(2,1)S(1)} %get-tuple-element.35), channel_id=1, source_target_pairs={{0,1},{1,2},{2,3},{3,4},{4,5},{5,6},{6,7},{7,8},{8,9},{9,10},{10,1... | collective-permute-start | bytes 393224 | tf_op jit(solution)/shard_map/ppermute | solution.py:28
  11.9 2.3 %copy-start.2 = (bf16[512,9,512]{2,0,1:T(8,128)(2,1)S(1)}, bf16[512,9,512]{2,0,1:T(8,128)(2,1)}, u32[]{:S(2)}) copy-start(bf16[512,9,512]{2,0,1:T(8,128)(2,1)} %param.6) | copy-start | bytes 14155780
  12.4 2.8 %copy-start.1 = (bf16[2,4,64,512]{3,2,1,0:T(8,128)(2,1)S(1)}, bf16[2,4,64,512]{3,2,1,0:T(8,128)(2,1)}, u32[]{:S(2)}) copy-start(bf16[2,4,64,512]{3,2,1,0:T(8,128)(2,1)} %param.4) | copy-start | bytes 1572868
  18.9 8.2 %collective-permute-start.3 = (bf16[2,1,64,512]{3,2,1,0:T(8,128)(2,1)S(1)}, bf16[2,1,64,512]{3,2,1,0:T(8,128)(2,1)S(1)}, u32[]{:S(2)}, u32[]{:S(2)}) collective-permute-start(bf16[2,1,64,512]{3,2,1,0:T(8,128)(2,1)S(1)} %get-tuple-element.32), channel_id=1, source_target_pairs={{1,0},{2,1},{3,2},{4,3},{5,4},{6,5},{7,6},{8,7},{9,8},{10,9},{11,1... | collective-permute-start | bytes 393224 | tf_op jit(solution)/shard_map/ppermute | solution.py:29
  20.8 6.3 %collective-permute-start.2 = (bf16[2,1,64,512]{3,2,1,0:T(8,128)(2,1)S(1)}, bf16[2,1,64,512]{3,2,1,0:T(8,128)(2,1)S(1)}, u32[]{:S(2)}, u32[]{:S(2)}) collective-permute-start(bf16[2,1,64,512]{3,2,1,0:T(8,128)(2,1)S(1)} %get-tuple-element.31), channel_id=1, source_target_pairs={{0,1},{1,2},{2,3},{3,4},{4,5},{5,6},{6,7},{7,8},{8,9},{9,10},{10,1... | collective-permute-start | bytes 393224 | tf_op jit(solution)/shard_map/ppermute | solution.py:28
  25.9 2.6 %slice-start = ((s8[4718592]{0:T(1024)(128)(4,1)}), s8[4194304]{0:T(1024)(128)(4,1)S(1)}, s32[]{:S(2)}) async-start(s8[4718592]{0:T(1024)(128)(4,1)} %bitcast.116), calls=%async_computation | async-start | bytes 8388608
  27.1 1.7 %slice-start.1 = ((s8[4718592]{0:T(1024)(128)(4,1)}), s8[524288]{0:T(1024)(128)(4,1)S(1)}, s32[]{:S(2)}) async-start(s8[4718592]{0:T(1024)(128)(4,1)} %bitcast.116), calls=%async_computation.1 | async-start | bytes 1048576
  32.9 1.0 copy-start

commit v4 on v3

v4 whole, which is shorter than its diff:
```python
import functools

import jax
import jax.numpy as jnp
from jax import lax
from jax.experimental import pallas as pl
from jax.experimental.pallas import tpu as pltpu
from jax.sharding import PartitionSpec as P

MESH = pl.DeviceIdType.MESH
EPS2 = 0.1 * 0.1
INV_ROOT_TWO = 0.7071067811865476
INV_ROOT_TWOPI = 0.3989422804014327


SIZES = (4, 4, 1)
AROUND = [(dr, dq) for dr in (-1, 0, 1) for dq in (-1, 0, 1) if dr or dq]


def step_kernel(spread_ref, truth_ref, w1_hbm, w2_hbm, prog_ref, outa, outb, *scratch):
    (w1, w2, stage, base, state, hidden, cots, state_sib, hidden_sib, slope, fore, leaving, cc, cp, csib) = scratch[:15]
    (ct, sa, ra, sb, rb, ta, tra, tb, trb, um, uz, ur, fin) = scratch[15:28]
    (local, sibs, sibr, hsend, hrecv, asend, arecv, s1, r1, s2, r2, s3, r3, s5, r5) = scratch[28:]
    bf, f32 = jnp.bfloat16, jnp.float32
    member, rows = lax.axis_index("member"), lax.axis_index("rows")
    x, zh = member // 2, lax.rem(member, 2)
    y, z, c = rows // 8, lax.rem(rows // 2, 4), lax.rem(rows, 2)
    q = zh * 4 + x
    outs = (outa, outb)

    def at(px, pzh, py, pz, pc):
        return {"member": px * 2 + pzh, "rows": (py * 4 + pz) * 2 + pc}

    def holder(pq):
        return lax.rem(pq, 4) * 2 + pq // 4

    sibling = at(x, zh, y, z, 1 - c)

    def mate(k):
        return {"member": holder(lax.rem(q + k, 8)), "rows": rows}

    def near(dr, dq):
        return {"member": holder(lax.rem(q + dq + 8, 8)), "rows": lax.rem(rows + dr + 32, 32)}

    def along_y(k):
        return at(x, zh, lax.rem(y + k, 4), z, c)

    def along_x(k):
        return at(lax.rem(x + k, 4), zh, y, z, c)

    def cross_x(k):
        return at(lax.rem(x + k, 4), zh, y, z, 1 - c)

    ring = zh * 4 + z

    def along_z(k):
        to = lax.rem(ring + k, 8)
        return at(x, to // 4, y, lax.rem(to, 4), c)

    def send(src, dst, ssem, rsem, to):
        return pltpu.make_async_remote_copy(
            src_ref=src, dst_ref=dst, send_sem=ssem, recv_sem=rsem, device_id=to, device_id_type=MESH
        )

    load_w1 = pltpu.make_async_copy(w1_hbm, w1, local.at[0])
    load_w2 = pltpu.make_async_copy(w2_hbm, w2, local.at[1])
    load_w1.start()
    load_w2.start()

    barrier = pltpu.get_barrier_semaphore()
    peers = [sibling] + [mate(k) for k in range(1, 8)] + [along_z(k) for k in range(1, 8)]
    peers += [near(dr, dq) for dr, dq in AROUND]
    peers += [a(k) for a in (along_y, along_x, cross_x) for k in (1, 2, 3)]
    for p in peers:
        pl.semaphore_signal(barrier, inc=1, device_id=p, device_id_type=MESH)
    pl.semaphore_wait(barrier, len(peers))

    def meet(k):
        to = lax.rem(q + k, 8)
        return send(spread_ref.at[to], stage.at[member], asend.at[0, k], arecv.at[0, k], mate(k))

    def leave(k):
        to = holder(lax.rem(q + k, 8))
        return send(leaving.at[to], prog_ref.at[q], asend.at[1, k], arecv.at[1, k], mate(k))

    far_first = (4, 3, 5, 2, 6, 1, 7)
    for k in far_first:
        meet(k).start()
    stage[member] = spread_ref[q]

    def halo(n, buf, i):
        dr, dq = AROUND[i]

        def cut(step, size, low, high):
            return pl.ds(low, size) if step == 0 else pl.ds(high if step > 0 else low, 1)

        def edge(step, size):
            return pl.ds(1, size) if step == 0 else pl.ds(0 if step > 0 else size + 1, 1)

        return send(
            buf.at[cut(dr, 4, 1, 4), cut(dq, 8, 1, 8)],
            buf.at[edge(dr, 4), edge(dq, 8)],
            hsend.at[n, i],
            hrecv.at[n, i],
            near(dr, dq),
        )

    def halo_start(n, buf):
        for i in range(8):
            halo(n, buf, i).start()

    def halo_wait(n, buf):
        for i in range(8):
            halo(n, buf, i).wait_recv()

        @pl.when(rows == 0)
        def _():
            buf[0] = jnp.zeros((10, 16, 512), bf)

        @pl.when(rows == 31)
        def _():
            buf[5] = jnp.zeros((10, 16, 512), bf)

        @pl.when(q == 0)
        def _():
            for r in range(6):
                buf[r, 0] = jnp.zeros((16, 512), bf)

        @pl.when(q == 7)
        def _():
            for r in range(6):
                buf[r, 9] = jnp.zeros((16, 512), bf)

    def view(buf, down, across):
        return buf[pl.ds(down, 4), pl.ds(across, 8)].reshape(512, 512)

    def turned(value):
        return jnp.transpose(value.astype(f32), (1, 0)).astype(bf)

    mine = pl.multiple_of(c * 256, 256)
    theirs = pl.multiple_of((1 - c) * 256, 256)
    state_out = send(state, state_sib, sibs.at[0], sibr.at[0], sibling)
    hidden_out = send(hidden, hidden_sib, sibs.at[1], sibr.at[1], sibling)
    cot_out = send(cc.at[:, pl.ds(theirs, 256)], csib.at[0], sibs.at[2], sibr.at[2], sibling)
    pre_out = send(cp.at[:, pl.ds(theirs, 256)], csib.at[1], sibs.at[3], sibr.at[3], sibling)

    def step1(g, part, h, k):
        s, r = (sa, ra) if h == 0 else (sb, rb)
        to = lax.rem((y if h == 0 else x) + k, 4)
        taps = pl.ds(part * 4, SIZES[part])
        return send(
            s.at[g, to, taps],
            r.at[g, k - 1, taps],
            s1.at[g, part * 2 + h, k],
            r1.at[g, part * 2 + h, k],
            along_y(k) if h == 0 else along_x(k),
        )

    def step2(g, part, h, k):
        s, r = (ta, tra) if h == 0 else (tb, trb)
        to = lax.rem((x if h == 0 else y) + k, 4)
        taps = pl.ds(part * 4, SIZES[part])
        return send(
            s.at[g, to, taps],
            r.at[g, k - 1, taps],
            s2.at[g, part * 2 + h, k],
            r2.at[g, part * 2 + h, k],
            along_x(k) if h == 0 else along_y(k),
        )

    def step3(g, part, k):
        to = lax.rem(lax.rem(ring + k, 8), 4)
        pairs = pl.ds(part * 2, (SIZES[part] + 1) // 2)
        return send(uz.at[g, to, pairs], ur.at[g, ring, pairs], s3.at[g, part, k], r3.at[g, part, k], along_z(k))

    spot = c * 4 + x

    def step5(g, k, cross):
        pc = (1 - c) if cross else c
        to = (cross_x(k) if k else sibling) if cross else along_x(k)
        i = k + 4 * cross
        return send(um.at[g, pc], fin.at[g, spot], s5.at[g, i], r5.at[g, i], to)

    every5 = [(k, 0) for k in (2, 1, 3)] + [(k, 1) for k in (2, 1, 3, 0)]

    def form(g, part, own, sib):
        @pl.loop(part * 4, part * 4 + SIZES[part])
        def _(tap):
            down, across = tap // 3, lax.rem(tap, 3)
            total = jnp.dot(ct[0], view(own, down, across), preferred_element_type=f32)
            total = total + jnp.dot(ct[1], view(sib, down, across), preferred_element_type=f32)
            total = total.astype(bf)
            for xx in range(4):
                for yy in range(4):
                    for h in range(2):
                        top = xx * 64 + h * 32
                        piece = total[top : top + 32, yy * 128 : yy * 128 + 128]
                        if h == 0:
                            sa[g, yy, tap, xx] = piece
                        else:
                            sb[g, xx, tap, yy] = piece

        for k in (2, 1, 3):
            step1(g, part, 0, k).start()
            step1(g, part, 1, k).start()

    def summed(own, got, where):
        total = own[where].astype(f32)
        for k in range(3):
            total = total + got[(k,) + where].astype(f32)
        return total

    def add1(g, part):
        for h in range(2):
            for k in (1, 2, 3):
                step1(g, part, h, k).wait_recv()
            own, got, into = ((sa, ra, ta), (sb, rb, tb))[h]
            here = y if h == 0 else x

            @pl.loop(part * 4, part * 4 + SIZES[part])
            def _(tap):
                total = summed(own.at[g, here], got.at[g], (tap,)).astype(bf)
                for other in range(4):
                    into[g, other, tap] = total[other]

            for k in (2, 1, 3):
                step2(g, part, h, k).start()

    def add2(g, part):
        for h in range(2):
            for k in (1, 2, 3):
                step2(g, part, h, k).wait_recv()
        for pair in range(part * 2, part * 2 + (SIZES[part] + 1) // 2):
            blocks = []
            for tap in (2 * pair, 2 * pair + 1):
                for h in range(2):
                    own, got = ((ta, tra), (tb, trb))[h]
                    here = x if h == 0 else y
                    blocks.append(
                        summed(own.at[g, here], got.at[g], (tap,)) if tap < 9 else jnp.zeros((32, 128), f32)
                    )
            flat = jnp.transpose(jnp.concatenate(blocks, axis=0), (1, 0)).astype(bf)
            for zz in range(4):
                uz[g, zz, pair] = flat[zz * 32 : zz * 32 + 32]
        for k in (4, 3, 5, 2, 6, 1, 7):
            step3(g, part, k).start()
        pairs = pl.ds(part * 2, (SIZES[part] + 1) // 2)
        ur[g, ring, pairs] = uz[g, z, pairs]

    def add3(g, part):
        for k in range(1, 8):
            step3(g, part, k).wait_recv()
        pairs = slice(part * 2, part * 2 + (SIZES[part] + 1) // 2)
        total = ur[g, 0, pairs].astype(f32)
        for q in range(1, 8):
            total = total + ur[g, q, pairs].astype(f32)
        total = total.astype(bf)
        um[g, 0, pairs] = total[:, :16]
        um[g, 1, pairs] = total[:, 16:]

    def spread(g):
        for k, cross in every5:
            step5(g, k, cross).start()
        fin[g, spot] = um[g, c]

    def finish(g):
        for k, cross in every5:
            step5(g, k, cross).wait_recv()
        for tap in range(9):
            off = (tap % 2) * 64
            row = [fin[g, i, tap // 2, :, off : off + 64].astype(f32) for i in range(8)]
            outs[g][tap] = jnp.concatenate(row, axis=1)

    for k in range(1, 8):
        meet(k).wait_recv()

    @pl.loop(0, 8)
    def _(m):
        for j in range(2):
            for l in range(4):
                lanes = slice(l * 128, l * 128 + 128)
                value = stage[m, j * 32 : j * 32 + 32, lanes].astype(f32)
                base[l, pl.ds(m * 2 + j, 32, stride=16), :] = value

    for l in range(4):
        state[1:5, 1:9, :, l * 128 : l * 128 + 128] = base[l].astype(bf).reshape(4, 8, 16, 128)
    halo_start(0, state)
    load_w1.wait()
    halo_wait(0, state)
    state_out.start()

    def conv(buf, w, half):
        total = None
        for tap in range(9):
            term = jnp.dot(
                view(buf, tap // 3, tap % 3), w[tap, :, half * 256 : half * 256 + 256], preferred_element_type=f32
            )
            total = term if total is None else total + term
        return total

    for half in range(2):
        lanes = slice(half * 256, half * 256 + 256)
        pre = conv(state, w1, half)
        both = 0.5 * (1.0 + lax.erf(pre * INV_ROOT_TWO))
        slope[:, lanes] = both + pre * jnp.exp(-0.5 * pre * pre) * INV_ROOT_TWOPI
        hidden[1:5, 1:9, :, lanes] = (pre * both).astype(bf).reshape(4, 8, 16, 256)

    halo_start(1, hidden)
    load_w2.wait()
    halo_wait(1, hidden)
    hidden_out.start()
    for half in range(2):
        total = conv(hidden, w2, half)
        for l in range(2):
            fore[half * 2 + l] = base[half * 2 + l] + total[:, l * 128 : l * 128 + 128]

    for l in range(4):
        for k in range(16):
            value = fore[l, pl.ds(k, 32, stride=16), :]
            leaving[k // 2, (k % 2) * 32 : (k % 2) * 32 + 32, l * 128 : l * 128 + 128] = value.astype(bf)

    @pl.loop(0, 4)
    def _(l):
        @pl.loop(0, 4)
        def _(cell):
            truth = truth_ref[q, l, pl.ds(pl.multiple_of(cell * 8, 8), 8), :]

            def spot_of(k):
                return pl.ds(cell * 128 + k, 8, stride=16)

            xs = [fore[l, spot_of(k), :] for k in range(16)]
            pulls = [None] * 16

            def plus(i, v):
                pulls[i] = v if pulls[i] is None else pulls[i] + v

            for a in range(16):
                for b in range(a + 1, 16):
                    d = xs[a] - xs[b]
                    u = d * lax.rsqrt(d * d + EPS2)
                    plus(a, u)
                    plus(b, -u)
            for k in range(16):
                d = xs[k] - truth
                away = d * lax.rsqrt(d * d + EPS2)
                fore[l, spot_of(k), :] = away * (1.0 / 2048.0) - pulls[k] * (1.0 / 30720.0)

    for l in range(4):
        lanes = slice(l * 128, l * 128 + 128)
        value = fore[l].astype(bf)
        cc[:, lanes] = value
        cots[1:5, 1:9, :, lanes] = value.reshape(4, 8, 16, 128)
    cot_out.start()
    halo_start(2, cots)
    for k in far_first:
        leave(k).start()
    prog_ref[q] = leaving[member]

    ct[0] = turned(cc[:, pl.ds(mine, 256)])
    cot_out.wait_recv()
    ct[1] = turned(csib[0])
    hidden_out.wait_recv()
    for part in range(3):
        form(0, part, hidden, hidden_sib)

    halo_wait(2, cots)
    for half in range(2):
        lanes = pl.ds(half * 256, 256)
        total = None
        for tap in range(9):
            term = lax.dot_general(
                view(cots, 2 - tap // 3, 2 - tap % 3),
                w2[tap, lanes],
                (((1,), (1,)), ((), ())),
                preferred_element_type=f32,
            )
            total = term if total is None else total + term
        cp[:, lanes] = (total * slope[:, lanes]).astype(bf)

    pre_out.start()
    ct[0] = turned(cp[:, pl.ds(mine, 256)])
    pre_out.wait_recv()
    ct[1] = turned(csib[1])
    state_out.wait_recv()
    add1(0, 0)
    form(1, 0, state, state_sib)
    add1(0, 1)
    form(1, 1, state, state_sib)
    add2(0, 0)
    form(1, 2, state, state_sib)
    add1(0, 2)
    add2(0, 1)
    add2(0, 2)
    add1(1, 0)
    add3(0, 0)
    add3(0, 1)
    add3(0, 2)
    spread(0)
    add2(1, 0)
    add1(1, 1)
    add1(1, 2)
    add2(1, 1)
    add2(1, 2)
    finish(0)
    add3(1, 0)
    add3(1, 1)
    add3(1, 2)
    spread(1)
    finish(1)

    for k in range(1, 8):
        meet(k).wait_send()
        leave(k).wait()
    for copy in (state_out, hidden_out, cot_out, pre_out):
        copy.wait_send()
    for n, buf in enumerate((state, hidden, cots)):
        for i in range(8):
            halo(n, buf, i).wait_send()
    for g in range(2):
        for part in range(3):
            for k in (1, 2, 3):
                for h in range(2):
                    step1(g, part, h, k).wait_send()
                    step2(g, part, h, k).wait_send()
            for k in range(1, 8):
                step3(g, part, k).wait_send()
        for k, cross in every5:
            step5(g, k, cross).wait_send()


def whole_step(spread, truth, first, second):
    bf, f32 = jnp.bfloat16, jnp.float32
    dma = pltpu.SemaphoreType.DMA
    vmem = pltpu.VMEM
    pair = [vmem((2, 4, 9, 4, 32, 128), bf), vmem((2, 3, 9, 4, 32, 128), bf)]
    quad = [vmem((2, 4, 9, 32, 128), bf), vmem((2, 3, 9, 32, 128), bf)]
    block = vmem((6, 10, 16, 512), bf)
    scratch = [
        vmem((9, 512, 512), bf),
        vmem((9, 512, 512), bf),
        vmem((8, 64, 512), bf),
        vmem((4, 512, 128), f32),
        block,
        block,
        block,
        block,
        block,
        vmem((512, 512), f32),
        vmem((4, 512, 128), f32),
        vmem((8, 64, 512), bf),
        vmem((512, 512), bf),
        vmem((512, 512), bf),
        vmem((2, 512, 256), bf),
        vmem((2, 256, 512), bf),
    ]
    scratch += pair + pair + quad + quad
    scratch += [
        vmem((2, 2, 5, 16, 128), bf),
        vmem((2, 4, 5, 32, 128), bf),
        vmem((2, 8, 5, 32, 128), bf),
        vmem((2, 8, 5, 16, 128), bf),
    ]
    scratch += [dma((2,)), dma((4,)), dma((4,)), dma((3, 8)), dma((3, 8)), dma((2, 8)), dma((2, 8))]
    for dims in ((2, 6, 4), (2, 6, 4), (2, 3, 8), (2, 8)):
        scratch += [dma(dims), dma(dims)]
    in_vmem = pl.BlockSpec(memory_space=pltpu.VMEM)
    return pl.pallas_call(
        step_kernel,
        out_shape=[jax.ShapeDtypeStruct((8, 64, 512), bf)] + [jax.ShapeDtypeStruct((9, 16, 512), f32)] * 2,
        in_specs=[in_vmem] * 2 + [pl.BlockSpec(memory_space=pl.ANY)] * 2,
        out_specs=[in_vmem] * 3,
        scratch_shapes=scratch,
        compiler_params=pltpu.CompilerParams(collective_id=0, has_side_effects=True, vmem_limit_bytes=60 << 20),
        name="whole_step",
    )(spread, truth, first, second)


def body(state, truth, conv_first, conv_second):
    members, rows, cols, channels = state.shape
    width = cols // 8
    spread = state.reshape(members, rows, 8, width, channels).transpose(2, 0, 1, 3, 4)
    facts = truth.astype(jnp.float32).reshape(rows, 8, width, channels // 128, 128).transpose(1, 3, 0, 2, 4)
    prognosis, second_slope, first_slope = whole_step(
        spread.reshape(8, members * rows * width, channels),
        facts.reshape(8, channels // 128, rows * width, 128),
        jnp.transpose(conv_first, (1, 0, 2)),
        jnp.transpose(conv_second, (1, 0, 2)),
    )
    prognosis = prognosis.reshape(8, members, rows, width, channels).transpose(1, 2, 0, 3, 4).reshape(state.shape)
    return prognosis, jnp.transpose(first_slope, (1, 0, 2)), jnp.transpose(second_slope, (1, 0, 2))


def solution(mesh):
    in_specs = (P("member", "rows", None, None), P("rows", None, None), P(), P())
    out_specs = (P("member", "rows", None, None), P("rows", None, None), P("rows", None, None))
    return jax.shard_map(body, mesh=mesh, in_specs=in_specs, out_specs=out_specs, check_vma=False)
```

time: 160 us -> 135 us (0.84)
  starting transfers between devices: 13.3 us -> 0 us
  matrix products: 7.92 us -> 0 us
  Pallas kernels: 118 us -> 125 us
  other arithmetic: 6.32 us -> 1.8 us
  local copies, waits for them, and re-layouts: 11.2 us -> 7.16 us
  waiting for transfers between devices: 1.93 us -> 0 us
    ppermute x4 -> x0, starting transfers between devices: 13.3 us -> none  [the longest x2 7.07 us: padded(): high = lax.ppermute(field[:, :1], 'rows', backward)]
    dot_general x18 -> x0, matrix products: 7.92 us -> none  [conv(): jnp.dot(tap_view(pad, tap, rows, cols), kernel[:, tap, :], preferred_elem...]
    pallas_call x2 -> x1, Pallas kernels: 118 us -> 125 us  [whole_step(): pl.pallas_call(step_kernel, out_shape=[jax.ShapeDtypeStruct((8, 64, 512),...]
    slice x12 -> x0, local copies, waits for them, and re-layouts: 3.08 us -> none  [the longest x8 1.18 us: column_shifts(): ordered[:, :, b:b + cols].reshape(-1, pad.shape[3])]
    unnamed x12 -> x2, local copies, waits for them, and re-layouts: 6.24 us -> 3.39 us
    another operation x1 -> x0, other arithmetic: 2.64 us -> none  [column_shifts(): jnp.stack([ordered[:, :, b:b + cols].reshape(-1, pad.shape[3]) for b in r...]
    ppermute x4 -> x0, waiting for transfers between devices: 1.93 us -> none  [the longest x2 1.43 us: padded(): low = lax.ppermute(field[:, -1:], 'rows', forward)]
    reshape x0 -> x1, other arithmetic: none -> 1.8 us  [body(): facts.reshape(8, channels // 128, rows * width, 128)]
  transfers between devices with their start and end apart: 4 -> 0, of which waited for: 2 -> 0; matrix products, arithmetic and copies ran while one was open for 1% -> 0% of each run, Pallas kernels for 0% -> 0%
where the time goes in v4:
time: 135 us
  Pallas kernels  125 us (93%)
  local copies, waits for them, and re-layouts  7.16 us (5%)
  other arithmetic  1.8 us (1%)
    pallas_call x1, Pallas kernels, whole_step(): pl.pallas_call(step_kernel, out_shape=[jax.ShapeDtypeStruct((8, 64, 512),...  125 us
    unnamed x2, local copies, waits for them, and re-layouts  3.39 us

profile of v4, /device:TPU:1, one launch (start us, length us, event | category | flops | bytes accessed | tf_op | source)
XLA Modules:
  0.0 134.6 jit_solution(13639718359688242303)
XLA Ops:
  0.6 1.9 %copy.7 = bf16[2,4,8,8,512]{4,3,1,0,2:T(8,128)(2,1)} copy(bf16[2,4,8,8,512]{4,3,2,1,0:T(8,128)(2,1)} %bitcast.25) | data formatting | bytes 1048576 | tf_op jit(solution)/shard_map/reshape | solution.py:481
  2.5 1.8 %copy_bitcast_fusion.1.truth_ref = f32[8,4,32,128]{3,2,1,0:T(8,128)} fusion(bf16[4,64,512]{2,1,0:T(8,128)(2,1)} %param.5), kind=kLoop, calls=%fused_computation.1 | loop fusion | flops 131072 | bytes 786432 | tf_op jit(solution)/shard_map/reshape | solution.py:485
  4.3 125.0 %whole_step.1 = (bf16[8,64,512]{2,1,0:T(8,128)(2,1)}, f32[9,16,512]{2,1,0:T(8,128)}, f32[9,16,512]{2,1,0:T(8,128)}) custom-call(bf16[8,64,512]{2,1,0:T(8,128)(2,1)} %bitcast.24, f32[8,4,32,128]{3,2,1,0:T(8,128)} %copy_bitcast_fusion.1.truth_ref, bf16[9,512,512]{2,1,0:T(8,128)(2,1)} %bitcast.22, bf16[9,512,512]{2,1,0:T(8,128)(2,1)} %bitcast.23), custom_call_target="tpu_custom_call" | custom-call | tf_op jit(solution)/shard_map/whole_step/pallas_call | solution.py:467
  129.3 1.9 %copy.12 = bf16[2,4,8,8,512]{4,3,2,1,0:T(8,128)(2,1)} copy(bf16[2,4,8,8,512]{4,3,1,0,2:T(8,128)(2,1)} %bitcast.27) | data formatting | bytes 1048576 | tf_op jit(solution)/shard_map/transpose | solution.py:489
  131.2 1.7 %copy.15 = f32[16,9,512]{2,0,1:T(8,128)} copy(f32[16,9,512]{2,0,1:T(8,128)} %bitcast.29) | data formatting | bytes 589824
  132.9 1.7 %copy.16 = f32[16,9,512]{2,0,1:T(8,128)} copy(f32[16,9,512]{2,0,1:T(8,128)} %bitcast.28) | data formatting | bytes 589824

commit v5 on v4

--- a/solution.py
+++ b/solution.py
@@ -14,19 +14,20 @@
 
 
 SIZES = (4, 4, 1)
+WIDE = 40
+HEIGHT = (WIDE, 64 - WIDE)
 AROUND = [(dr, dq) for dr in (-1, 0, 1) for dq in (-1, 0, 1) if dr or dq]
 
 
-def step_kernel(spread_ref, truth_ref, w1_hbm, w2_hbm, prog_ref, outa, outb, *scratch):
-    (w1, w2, stage, base, state, hidden, cots, state_sib, hidden_sib, slope, fore, leaving, cc, cp, csib) = scratch[:15]
-    (ct, sa, ra, sb, rb, ta, tra, tb, trb, um, uz, ur, fin) = scratch[15:28]
-    (local, sibs, sibr, hsend, hrecv, asend, arecv, s1, r1, s2, r2, s3, r3, s5, r5) = scratch[28:]
+def step_kernel(state_hbm, truth_hbm, w1_hbm, w2_hbm, prog_ref, out_ref, *scratch):
+    (w1, w2, stage, base, state, hidden, cots, state_sib, hidden_sib, slope, fore, leaving, cc, cp, csib, truth) = scratch[:16]
+    (ct, sa, ra, sb, rb, ta, tra, tb, trb, um, uz, ur, fin) = scratch[16:29]
+    (local, sibs, sibr, hsend, hrecv, asend, arecv, s1, r1, s2, r2, s3, r3, s5, r5) = scratch[29:]
     bf, f32 = jnp.bfloat16, jnp.float32
     member, rows = lax.axis_index("member"), lax.axis_index("rows")
     x, zh = member // 2, lax.rem(member, 2)
     y, z, c = rows // 8, lax.rem(rows // 2, 4), lax.rem(rows, 2)
     q = zh * 4 + x
-    outs = (outa, outb)
 
     def at(px, pzh, py, pz, pc):
         return {"member": px * 2 + pzh, "rows": (py * 4 + pz) * 2 + pc}
@@ -68,16 +69,22 @@
     load_w2.start()
 
     barrier = pltpu.get_barrier_semaphore()
-    peers = [sibling] + [mate(k) for k in range(1, 8)] + [along_z(k) for k in range(1, 8)]
-    peers += [near(dr, dq) for dr, dq in AROUND]
-    peers += [a(k) for a in (along_y, along_x, cross_x) for k in (1, 2, 3)]
+    peers = [mate(k) for k in range(1, 8)] + [along_z(k) for k in (1, 2, 3, 5, 6, 7)]
+    peers += [near(dr, dq) for dr, dq in AROUND if dr]
+    peers += [a(k) for a in (along_y, cross_x) for k in (1, 2, 3)]
     for p in peers:
         pl.semaphore_signal(barrier, inc=1, device_id=p, device_id_type=MESH)
     pl.semaphore_wait(barrier, len(peers))
 
+    def columns(pq):
+        return pl.ds(pl.multiple_of(pq * 8, 8), 8)
+
+    own_state = pltpu.make_async_copy(state_hbm.at[:, :, columns(q)], stage.at[member], local.at[2])
+    own_truth = pltpu.make_async_copy(truth_hbm.at[:, columns(q)], truth, local.at[3])
+
     def meet(k):
         to = lax.rem(q + k, 8)
-        return send(spread_ref.at[to], stage.at[member], asend.at[0, k], arecv.at[0, k], mate(k))
+        return send(state_hbm.at[:, :, columns(to)], stage.at[member], asend.at[0, k], arecv.at[0, k], mate(k))
 
     def leave(k):
         to = holder(lax.rem(q + k, 8))
@@ -86,7 +93,8 @@
     far_first = (4, 3, 5, 2, 6, 1, 7)
     for k in far_first:
         meet(k).start()
-    stage[member] = spread_ref[q]
+    own_state.start()
+    own_truth.start()
 
     def halo(n, buf, i):
         dr, dq = AROUND[i]
@@ -105,13 +113,29 @@
             near(dr, dq),
         )
 
+    def inside(dr, dq):
+        there = None
+        for ok in [rows > 0] * (dr < 0) + [rows < 31] * (dr > 0) + [q > 0] * (dq < 0) + [q < 7] * (dq > 0):
+            there = ok if there is None else jnp.logical_and(there, ok)
+        return there
+
     def halo_start(n, buf):
-        for i in range(8):
-            halo(n, buf, i).start()
+        for i, (dr, dq) in enumerate(AROUND):
+            @pl.when(inside(dr, dq))
+            def _():
+                halo(n, buf, i).start()
+
+    def halo_sent(n, buf):
+        for i, (dr, dq) in enumerate(AROUND):
+            @pl.when(inside(dr, dq))
+            def _():
+                halo(n, buf, i).wait_send()
 
     def halo_wait(n, buf):
-        for i in range(8):
-            halo(n, buf, i).wait_recv()
+        for i, (dr, dq) in enumerate(AROUND):
+            @pl.when(inside(-dr, -dq))
+            def _():
+                halo(n, buf, i).wait_recv()
 
         @pl.when(rows == 0)
         def _():
@@ -189,12 +213,11 @@
             down, across = tap // 3, lax.rem(tap, 3)
             total = jnp.dot(ct[0], view(own, down, across), preferred_element_type=f32)
             total = total + jnp.dot(ct[1], view(sib, down, across), preferred_element_type=f32)
-            total = total.astype(bf)
             for xx in range(4):
                 for yy in range(4):
                     for h in range(2):
-                        top = xx * 64 + h * 32
-                        piece = total[top : top + 32, yy * 128 : yy * 128 + 128]
+                        top = xx * 64 + h * WIDE
+                        piece = total[top : top + HEIGHT[h], yy * 128 : yy * 128 + 128].astype(bf)
                         if h == 0:
                             sa[g, yy, tap, xx] = piece
                         else:
@@ -237,7 +260,7 @@
                     own, got = ((ta, tra), (tb, trb))[h]
                     here = x if h == 0 else y
                     blocks.append(
-                        summed(own.at[g, here], got.at[g], (tap,)) if tap < 9 else jnp.zeros((32, 128), f32)
+                        summed(own.at[g, here], got.at[g], (tap,)) if tap < 9 else jnp.zeros((HEIGHT[h], 128), f32)
                     )
             flat = jnp.transpose(jnp.concatenate(blocks, axis=0), (1, 0)).astype(bf)
             for zz in range(4):
@@ -268,9 +291,10 @@
             step5(g, k, cross).wait_recv()
         for tap in range(9):
             off = (tap % 2) * 64
-            row = [fin[g, i, tap // 2, :, off : off + 64].astype(f32) for i in range(8)]
-            outs[g][tap] = jnp.concatenate(row, axis=1)
-
+            row = [fin[g, i, tap // 2, :, off : off + 64] for i in range(8)]
+            out_ref[g, tap] = jnp.concatenate(row, axis=1)
+
+    own_state.wait()
     for k in range(1, 8):
         meet(k).wait_recv()
 
@@ -279,7 +303,7 @@
         for j in range(2):
             for l in range(4):
                 lanes = slice(l * 128, l * 128 + 128)
-                value = stage[m, j * 32 : j * 32 + 32, lanes].astype(f32)
+                value = stage[m, j, :, :, lanes].astype(f32).reshape(32, 128)
                 base[l, pl.ds(m * 2 + j, 32, stride=16), :] = value
 
     for l in range(4):
@@ -319,11 +343,13 @@
             value = fore[l, pl.ds(k, 32, stride=16), :]
             leaving[k // 2, (k % 2) * 32 : (k % 2) * 32 + 32, l * 128 : l * 128 + 128] = value.astype(bf)
 
+    own_truth.wait()
+
     @pl.loop(0, 4)
     def _(l):
         @pl.loop(0, 4)
         def _(cell):
-            truth = truth_ref[q, l, pl.ds(pl.multiple_of(cell * 8, 8), 8), :]
+            fact = truth[cell, :, pl.ds(pl.multiple_of(l * 128, 128), 128)].astype(f32)
 
             def spot_of(k):
                 return pl.ds(cell * 128 + k, 8, stride=16)
@@ -341,7 +367,7 @@
                     plus(a, u)
                     plus(b, -u)
             for k in range(16):
-                d = xs[k] - truth
+                d = xs[k] - fact
                 away = d * lax.rsqrt(d * d + EPS2)
                 fore[l, spot_of(k), :] = away * (1.0 / 2048.0) - pulls[k] * (1.0 / 30720.0)
 
@@ -352,9 +378,6 @@
         cots[1:5, 1:9, :, lanes] = value.reshape(4, 8, 16, 128)
     cot_out.start()
     halo_start(2, cots)
-    for k in far_first:
-        leave(k).start()
-    prog_ref[q] = leaving[member]
 
     ct[0] = turned(cc[:, pl.ds(mine, 256)])
     cot_out.wait_recv()
@@ -364,6 +387,9 @@
         form(0, part, hidden, hidden_sib)
 
     halo_wait(2, cots)
+    for k in far_first:
+        leave(k).start()
+    prog_ref[q] = leaving[member]
     for half in range(2):
         lanes = pl.ds(half * 256, 256)
         total = None
@@ -382,29 +408,22 @@
     pre_out.wait_recv()
     ct[1] = turned(csib[1])
     state_out.wait_recv()
-    add1(0, 0)
-    form(1, 0, state, state_sib)
-    add1(0, 1)
-    form(1, 1, state, state_sib)
-    add2(0, 0)
-    form(1, 2, state, state_sib)
-    add1(0, 2)
-    add2(0, 1)
-    add2(0, 2)
-    add1(1, 0)
-    add3(0, 0)
-    add3(0, 1)
-    add3(0, 2)
+    for part in range(3):
+        add1(0, part)
+    for part in range(3):
+        form(1, part, state, state_sib)
+    for part in range(3):
+        add2(0, part)
+    for part in range(3):
+        add3(0, part)
     spread(0)
-    add2(1, 0)
-    add1(1, 1)
-    add1(1, 2)
-    add2(1, 1)
-    add2(1, 2)
+    for part in range(3):
+        add1(1, part)
+    for part in range(3):
+        add2(1, part)
     finish(0)
-    add3(1, 0)
-    add3(1, 1)
-    add3(1, 2)
+    for part in range(3):
+        add3(1, part)
     spread(1)
     finish(1)
 
@@ -414,8 +433,7 @@
     for copy in (state_out, hidden_out, cot_out, pre_out):
         copy.wait_send()
     for n, buf in enumerate((state, hidden, cots)):
-        for i in range(8):
-            halo(n, buf, i).wait_send()
+        halo_sent(n, buf)
     for g in range(2):
         for part in range(3):
             for k in (1, 2, 3):
@@ -428,17 +446,15 @@
             step5(g, k, cross).wait_send()
 
 
-def whole_step(spread, truth, first, second):
+def whole_step(state, truth, first, second):
     bf, f32 = jnp.bfloat16, jnp.float32
     dma = pltpu.SemaphoreType.DMA
     vmem = pltpu.VMEM
-    pair = [vmem((2, 4, 9, 4, 32, 128), bf), vmem((2, 3, 9, 4, 32, 128), bf)]
-    quad = [vmem((2, 4, 9, 32, 128), bf), vmem((2, 3, 9, 32, 128), bf)]
     block = vmem((6, 10, 16, 512), bf)
     scratch = [
         vmem((9, 512, 512), bf),
         vmem((9, 512, 512), bf),
-        vmem((8, 64, 512), bf),
+        vmem((8, 2, 4, 8, 512), bf),
         vmem((4, 512, 128), f32),
         block,
         block,
@@ -451,43 +467,42 @@
         vmem((512, 512), bf),
         vmem((512, 512), bf),
         vmem((2, 512, 256), bf),
+        vmem((4, 8, 512), bf),
         vmem((2, 256, 512), bf),
     ]
-    scratch += pair + pair + quad + quad
+    for height in HEIGHT:
+        scratch += [vmem((2, 4, 9, 4, height, 128), bf), vmem((2, 3, 9, 4, height, 128), bf)]
+    for height in HEIGHT:
+        scratch += [vmem((2, 4, 9, height, 128), bf), vmem((2, 3, 9, height, 128), bf)]
     scratch += [
         vmem((2, 2, 5, 16, 128), bf),
         vmem((2, 4, 5, 32, 128), bf),
         vmem((2, 8, 5, 32, 128), bf),
         vmem((2, 8, 5, 16, 128), bf),
     ]
-    scratch += [dma((2,)), dma((4,)), dma((4,)), dma((3, 8)), dma((3, 8)), dma((2, 8)), dma((2, 8))]
+    scratch += [dma((4,)), dma((4,)), dma((4,)), dma((3, 8)), dma((3, 8)), dma((2, 8)), dma((2, 8))]
     for dims in ((2, 6, 4), (2, 6, 4), (2, 3, 8), (2, 8)):
         scratch += [dma(dims), dma(dims)]
     in_vmem = pl.BlockSpec(memory_space=pltpu.VMEM)
     return pl.pallas_call(
         step_kernel,
-        out_shape=[jax.ShapeDtypeStruct((8, 64, 512), bf)] + [jax.ShapeDtypeStruct((9, 16, 512), f32)] * 2,
-        in_specs=[in_vmem] * 2 + [pl.BlockSpec(memory_space=pl.ANY)] * 2,
-        out_specs=[in_vmem] * 3,
+        out_shape=[jax.ShapeDtypeStruct((8, 64, 512), bf), jax.ShapeDtypeStruct((2, 9, 16, 512), bf)],
+        in_specs=[pl.BlockSpec(memory_space=pl.ANY)] * 4,
+        out_specs=[in_vmem] * 2,
         scratch_shapes=scratch,
         compiler_params=pltpu.CompilerParams(collective_id=0, has_side_effects=True, vmem_limit_bytes=60 << 20),
         name="whole_step",
-    )(spread, truth, first, second)
+    )(state, truth, first, second)
 
 
 def body(state, truth, conv_first, conv_second):
     members, rows, cols, channels = state.shape
-    width = cols // 8
-    spread = state.reshape(members, rows, 8, width, channels).transpose(2, 0, 1, 3, 4)
-    facts = truth.astype(jnp.float32).reshape(rows, 8, width, channels // 128, 128).transpose(1, 3, 0, 2, 4)
-    prognosis, second_slope, first_slope = whole_step(
-        spread.reshape(8, members * rows * width, channels),
-        facts.reshape(8, channels // 128, rows * width, 128),
-        jnp.transpose(conv_first, (1, 0, 2)),
-        jnp.transpose(conv_second, (1, 0, 2)),
+    prognosis, slopes = whole_step(
+        state, truth, jnp.transpose(conv_first, (1, 0, 2)), jnp.transpose(conv_second, (1, 0, 2))
     )
-    prognosis = prognosis.reshape(8, members, rows, width, channels).transpose(1, 2, 0, 3, 4).reshape(state.shape)
-    return prognosis, jnp.transpose(first_slope, (1, 0, 2)), jnp.transpose(second_slope, (1, 0, 2))
+    prognosis = prognosis.reshape(8, members, rows, cols // 8, channels).transpose(1, 2, 0, 3, 4).reshape(state.shape)
+    slopes = jnp.transpose(slopes.astype(jnp.float32), (0, 2, 1, 3))
+    return prognosis, slopes[1], slopes[0]
 
 
 def solution(mesh):

time: 135 us -> 120 us (0.89)
  Pallas kernels: 125 us -> 116 us
  local copies, waits for them, and re-layouts: 7.16 us -> 2.75 us
    pallas_call x1, Pallas kernels: 125 us -> 116 us  [whole_step(): pl.pallas_call(step_kernel, out_shape=[jax.ShapeDtypeStruct((8, 64, 512),...]
    unnamed x2 -> x0, local copies, waits for them, and re-layouts: 3.39 us -> none
    reshape x1 -> x0, local copies, waits for them, and re-layouts: 1.89 us -> none  [body(): state.reshape(members, rows, 8, width, channels).transpose(2, 0, 1, 3, 4)]
    reshape x1 -> x0, other arithmetic: 1.8 us -> none  [body(): facts.reshape(8, channels // 128, rows * width, 128)]
where the time goes in v5:
time: 120 us
  Pallas kernels  116 us (97%)
  local copies, waits for them, and re-layouts  2.75 us (2%)
    pallas_call x1, Pallas kernels, whole_step(): pl.pallas_call(step_kernel, out_shape=[jax.ShapeDtypeStruct((8, 64, 512),...  116 us

profile of v5, /device:TPU:1, one launch (start us, length us, event | category | flops | bytes accessed | tf_op | source)
XLA Modules:
  0.0 120.2 jit_solution(548787917481204738)
XLA Ops:
  0.6 115.8 %whole_step.1 = (bf16[8,64,512]{2,1,0:T(8,128)(2,1)}, bf16[2,9,16,512]{3,2,1,0:T(8,128)(2,1)}) custom-call(bf16[2,4,64,512]{3,2,1,0:T(8,128)(2,1)} %state_hbm.1, bf16[4,64,512]{2,1,0:T(8,128)(2,1)} %truth_hbm.1, bf16[9,512,512]{2,1,0:T(8,128)(2,1)} %bitcast.14, bf16[9,512,512]{2,1,0:T(8,128)(2,1)} %bitcast.15), custom_call_target="tpu_custom_call" | custom-call | tf_op jit(solution)/shard_map/whole_step/pallas_call | solution.py:487
  116.4 1.9 %copy.9 = bf16[2,4,8,8,512]{4,3,2,1,0:T(8,128)(2,1)} copy(bf16[2,4,8,8,512]{4,3,1,0,2:T(8,128)(2,1)} %bitcast.17) | data formatting | bytes 1048576 | tf_op jit(solution)/shard_map/transpose | solution.py:503
  118.3 1.0 convert_bitcast_fusion
  119.3 0.9 slice_bitcast_fusion

commit v6 on v5

--- a/solution.py
+++ b/solution.py
@@ -13,10 +13,11 @@
 INV_ROOT_TWOPI = 0.3989422804014327
 
 
-SIZES = (4, 4, 1)
+STARTS = (0, 4, 6, 8)
+SIZES = (4, 2, 2, 1)
 WIDE = 40
 HEIGHT = (WIDE, 64 - WIDE)
-AROUND = [(dr, dq) for dr in (-1, 0, 1) for dq in (-1, 0, 1) if dr or dq]
+AROUND = [(0, -1), (0, 1), (-1, -1), (-1, 1), (1, -1), (1, 1), (-1, 0), (1, 0)]
 
 
 def step_kernel(state_hbm, truth_hbm, w1_hbm, w2_hbm, prog_ref, out_ref, *scratch):
@@ -168,22 +169,38 @@
     cot_out = send(cc.at[:, pl.ds(theirs, 256)], csib.at[0], sibs.at[2], sibr.at[2], sibling)
     pre_out = send(cp.at[:, pl.ds(theirs, 256)], csib.at[1], sibs.at[3], sibr.at[3], sibling)
 
-    def step1(g, part, h, k):
-        s, r = (sa, ra) if h == 0 else (sb, rb)
-        to = lax.rem((y if h == 0 else x) + k, 4)
-        taps = pl.ds(part * 4, SIZES[part])
+    def taps_of(part):
+        return pl.ds(STARTS[part], SIZES[part])
+
+    def pairs_of(part):
+        return pl.ds(STARTS[part] // 2, (SIZES[part] + 1) // 2)
+
+    def turn(h, s):
+        here = y if h == 0 else x
+        one, two = here + 1 - 2 * lax.rem(here, 2), 3 - here
+        return (one, two) if s == 0 else (two, one)
+
+    def on_axis(h, place):
+        return at(x, zh, place, z, c) if h == 0 else at(place, zh, y, z, c)
+
+    def step1(g, part, h, s, j):
+        src, dst = (sa, ra) if h == 0 else (sb, rb)
+        here = y if h == 0 else x
+        one, two = turn(h, s)
+        block = (one, lax.rem(here + 2, 4), two)[j]
+        i = part * 4 + h * 2 + s
         return send(
-            s.at[g, to, taps],
-            r.at[g, k - 1, taps],
-            s1.at[g, part * 2 + h, k],
-            r1.at[g, part * 2 + h, k],
-            along_y(k) if h == 0 else along_x(k),
+            src.at[g, block, taps_of(part), pl.ds(s * 2, 2)],
+            dst.at[g, j, taps_of(part), pl.ds(s * 2, 2)],
+            s1.at[g, i, j],
+            r1.at[g, i, j],
+            on_axis(h, two if j == 2 else one),
         )
 
     def step2(g, part, h, k):
         s, r = (ta, tra) if h == 0 else (tb, trb)
         to = lax.rem((x if h == 0 else y) + k, 4)
-        taps = pl.ds(part * 4, SIZES[part])
+        taps = taps_of(part)
         return send(
             s.at[g, to, taps],
             r.at[g, k - 1, taps],
@@ -194,21 +211,22 @@
 
     def step3(g, part, k):
         to = lax.rem(lax.rem(ring + k, 8), 4)
-        pairs = pl.ds(part * 2, (SIZES[part] + 1) // 2)
+        pairs = pairs_of(part)
         return send(uz.at[g, to, pairs], ur.at[g, ring, pairs], s3.at[g, part, k], r3.at[g, part, k], along_z(k))
 
     spot = c * 4 + x
 
-    def step5(g, k, cross):
+    def step5(g, piece, k, cross):
         pc = (1 - c) if cross else c
         to = (cross_x(k) if k else sibling) if cross else along_x(k)
         i = k + 4 * cross
-        return send(um.at[g, pc], fin.at[g, spot], s5.at[g, i], r5.at[g, i], to)
+        part = pl.ds(0, 4) if piece == 0 else pl.ds(4, 1)
+        return send(um.at[g, pc, part], fin.at[g, spot, part], s5.at[g, piece, i], r5.at[g, piece, i], to)
 
     every5 = [(k, 0) for k in (2, 1, 3)] + [(k, 1) for k in (2, 1, 3, 0)]
 
     def form(g, part, own, sib):
-        @pl.loop(part * 4, part * 4 + SIZES[part])
+        @pl.loop(STARTS[part], STARTS[part] + SIZES[part])
         def _(tap):
             down, across = tap // 3, lax.rem(tap, 3)
             total = jnp.dot(ct[0], view(own, down, across), preferred_element_type=f32)
@@ -223,9 +241,25 @@
                         else:
                             sb[g, xx, tap, yy] = piece
 
-        for k in (2, 1, 3):
-            step1(g, part, 0, k).start()
-            step1(g, part, 1, k).start()
+        for j in (1, 0):
+            for h in range(2):
+                for half in range(2):
+                    step1(g, part, h, half, j).start()
+
+    def relay1(g, part):
+        for h in range(2):
+            own, got = ((sa, ra), (sb, rb))[h]
+            for half in range(2):
+                step1(g, part, h, half, 1).wait_recv()
+                two = turn(h, half)[1]
+
+                @pl.loop(STARTS[part], STARTS[part] + SIZES[part])
+                def _(tap):
+                    spot = (tap, slice(half * 2, half * 2 + 2))
+                    total = own[(g, two) + spot].astype(f32) + got[(g, 1) + spot].astype(f32)
+                    own[(g, two) + spot] = total.astype(bf)
+
+                step1(g, part, h, half, 2).start()
 
     def summed(own, got, where):
         total = own[where].astype(f32)
@@ -235,14 +269,16 @@
 
     def add1(g, part):
         for h in range(2):
-            for k in (1, 2, 3):
-                step1(g, part, h, k).wait_recv()
+            for half in range(2):
+                step1(g, part, h, half, 0).wait_recv()
+                step1(g, part, h, half, 2).wait_recv()
             own, got, into = ((sa, ra, ta), (sb, rb, tb))[h]
             here = y if h == 0 else x
 
-            @pl.loop(part * 4, part * 4 + SIZES[part])
+            @pl.loop(STARTS[part], STARTS[part] + SIZES[part])
             def _(tap):
-                total = summed(own.at[g, here], got.at[g], (tap,)).astype(bf)
+                total = own[g, here, tap].astype(f32) + got[g, 0, tap].astype(f32) + got[g, 2, tap].astype(f32)
+                total = total.astype(bf)
                 for other in range(4):
                     into[g, other, tap] = total[other]
 
@@ -253,7 +289,7 @@
         for h in range(2):
             for k in (1, 2, 3):
                 step2(g, part, h, k).wait_recv()
-        for pair in range(part * 2, part * 2 + (SIZES[part] + 1) // 2):
+        for pair in range(STARTS[part] // 2, STARTS[part] // 2 + (SIZES[part] + 1) // 2):
             blocks = []
             for tap in (2 * pair, 2 * pair + 1):
                 for h in range(2):
@@ -267,13 +303,13 @@
                 uz[g, zz, pair] = flat[zz * 32 : zz * 32 + 32]
         for k in (4, 3, 5, 2, 6, 1, 7):
             step3(g, part, k).start()
-        pairs = pl.ds(part * 2, (SIZES[part] + 1) // 2)
+        pairs = pairs_of(part)
         ur[g, ring, pairs] = uz[g, z, pairs]
 
     def add3(g, part):
         for k in range(1, 8):
             step3(g, part, k).wait_recv()
-        pairs = slice(part * 2, part * 2 + (SIZES[part] + 1) // 2)
+        pairs = slice(STARTS[part] // 2, STARTS[part] // 2 + (SIZES[part] + 1) // 2)
         total = ur[g, 0, pairs].astype(f32)
         for q in range(1, 8):
             total = total + ur[g, q, pairs].astype(f32)
@@ -281,14 +317,16 @@
         um[g, 0, pairs] = total[:, :16]
         um[g, 1, pairs] = total[:, 16:]
 
-    def spread(g):
+    def spread(g, piece):
         for k, cross in every5:
-            step5(g, k, cross).start()
-        fin[g, spot] = um[g, c]
+            step5(g, piece, k, cross).start()
+        part = slice(0, 4) if piece == 0 else slice(4, 5)
+        fin[g, spot, part] = um[g, c, part]
 
     def finish(g):
-        for k, cross in every5:
-            step5(g, k, cross).wait_recv()
+        for piece in range(2):
+            for k, cross in every5:
+                step5(g, piece, k, cross).wait_recv()
         for tap in range(9):
             off = (tap % 2) * 64
             row = [fin[g, i, tap // 2, :, off : off + 64] for i in range(8)]
@@ -383,8 +421,9 @@
     cot_out.wait_recv()
     ct[1] = turned(csib[0])
     hidden_out.wait_recv()
-    for part in range(3):
+    for part in range(4):
         form(0, part, hidden, hidden_sib)
+    relay1(0, 0)
 
     halo_wait(2, cots)
     for k in far_first:
@@ -402,29 +441,46 @@
             )
             total = term if total is None else total + term
         cp[:, lanes] = (total * slope[:, lanes]).astype(bf)
+        for part in ((1, 2), (3,))[half]:
+            relay1(0, part)
 
     pre_out.start()
     ct[0] = turned(cp[:, pl.ds(mine, 256)])
+    add1(0, 0)
     pre_out.wait_recv()
     ct[1] = turned(csib[1])
     state_out.wait_recv()
-    for part in range(3):
-        add1(0, part)
-    for part in range(3):
-        form(1, part, state, state_sib)
-    for part in range(3):
+    form(1, 0, state, state_sib)
+    add1(0, 1)
+    form(1, 1, state, state_sib)
+    add1(0, 2)
+    add1(0, 3)
+    form(1, 2, state, state_sib)
+    form(1, 3, state, state_sib)
+    relay1(1, 0)
+    for part in range(4):
         add2(0, part)
-    for part in range(3):
+    relay1(1, 1)
+    relay1(1, 2)
+    relay1(1, 3)
+    add1(1, 0)
+    for part in range(4):
         add3(0, part)
-    spread(0)
-    for part in range(3):
-        add1(1, part)
-    for part in range(3):
-        add2(1, part)
-    finish(0)
+    spread(0, 0)
+    spread(0, 1)
+    add1(1, 1)
+    add2(1, 0)
+    add1(1, 2)
+    add2(1, 1)
+    add1(1, 3)
+    add2(1, 2)
+    add2(1, 3)
     for part in range(3):
         add3(1, part)
-    spread(1)
+    spread(1, 0)
+    finish(0)
+    add3(1, 3)
+    spread(1, 1)
     finish(1)
 
     for k in range(1, 8):
@@ -435,15 +491,18 @@
     for n, buf in enumerate((state, hidden, cots)):
         halo_sent(n, buf)
     for g in range(2):
-        for part in range(3):
-            for k in (1, 2, 3):
-                for h in range(2):
-                    step1(g, part, h, k).wait_send()
+        for part in range(4):
+            for h in range(2):
+                for half in range(2):
+                    for j in range(3):
+                        step1(g, part, h, half, j).wait_send()
+                for k in (1, 2, 3):
                     step2(g, part, h, k).wait_send()
             for k in range(1, 8):
                 step3(g, part, k).wait_send()
-        for k, cross in every5:
-            step5(g, k, cross).wait_send()
+        for piece in range(2):
+            for k, cross in every5:
+                step5(g, piece, k, cross).wait_send()
 
 
 def whole_step(state, truth, first, second):
@@ -481,7 +540,7 @@
         vmem((2, 8, 5, 16, 128), bf),
     ]
     scratch += [dma((4,)), dma((4,)), dma((4,)), dma((3, 8)), dma((3, 8)), dma((2, 8)), dma((2, 8))]
-    for dims in ((2, 6, 4), (2, 6, 4), (2, 3, 8), (2, 8)):
+    for dims in ((2, 16, 3), (2, 8, 4), (2, 4, 8), (2, 2, 8)):
         scratch += [dma(dims), dma(dims)]
     in_vmem = pl.BlockSpec(memory_space=pltpu.VMEM)
     return pl.pallas_call(

time: 120 us -> 117 us (0.975)
  Pallas kernels: 116 us -> 113 us
    pallas_call x1, Pallas kernels: 116 us -> 113 us  [whole_step(): pl.pallas_call(step_kernel, out_shape=[jax.ShapeDtypeStruct((8, 64, 512),...]
where the time goes in v6:
time: 117 us
  Pallas kernels  113 us (97%)
  local copies, waits for them, and re-layouts  2.75 us (2%)
    pallas_call x1, Pallas kernels, whole_step(): pl.pallas_call(step_kernel, out_shape=[jax.ShapeDtypeStruct((8, 64, 512),...  113 us

profile of v6, /device:TPU:1, one launch (start us, length us, event | category | flops | bytes accessed | tf_op | source)
XLA Modules:
  0.0 117.2 jit_solution(6578677713155957968)
XLA Ops:
  0.6 112.8 %whole_step.1 = (bf16[8,64,512]{2,1,0:T(8,128)(2,1)}, bf16[2,9,16,512]{3,2,1,0:T(8,128)(2,1)}) custom-call(bf16[2,4,64,512]{3,2,1,0:T(8,128)(2,1)} %state_hbm.1, bf16[4,64,512]{2,1,0:T(8,128)(2,1)} %truth_hbm.1, bf16[9,512,512]{2,1,0:T(8,128)(2,1)} %bitcast.14, bf16[9,512,512]{2,1,0:T(8,128)(2,1)} %bitcast.15), custom_call_target="tpu_custom_call" | custom-call | tf_op jit(solution)/shard_map/whole_step/pallas_call | solution.py:546
  113.5 1.9 %copy.9 = bf16[2,4,8,8,512]{4,3,2,1,0:T(8,128)(2,1)} copy(bf16[2,4,8,8,512]{4,3,1,0,2:T(8,128)(2,1)} %bitcast.17) | data formatting | bytes 1048576 | tf_op jit(solution)/shard_map/transpose | solution.py:562
  115.4 1.0 convert_bitcast_fusion
  116.4 0.9 slice_bitcast_fusion

commit v7 on v6

--- a/solution.py
+++ b/solution.py
@@ -38,8 +38,11 @@
 
     sibling = at(x, zh, y, z, 1 - c)
 
+    def block_of(k):
+        return lax.rem(x + k, 4) + 4 * (zh if k < 4 else 1 - zh)
+
     def mate(k):
-        return {"member": holder(lax.rem(q + k, 8)), "rows": rows}
+        return {"member": holder(block_of(k)), "rows": rows}
 
     def near(dr, dq):
         return {"member": holder(lax.rem(q + dq + 8, 8)), "rows": lax.rem(rows + dr + 32, 32)}
@@ -84,20 +87,21 @@
     own_truth = pltpu.make_async_copy(truth_hbm.at[:, columns(q)], truth, local.at[3])
 
     def meet(k):
-        to = lax.rem(q + k, 8)
+        to = block_of(k)
         return send(state_hbm.at[:, :, columns(to)], stage.at[member], asend.at[0, k], arecv.at[0, k], mate(k))
 
     def leave(k):
-        to = holder(lax.rem(q + k, 8))
+        to = holder(block_of(k))
         return send(leaving.at[to], prog_ref.at[q], asend.at[1, k], arecv.at[1, k], mate(k))
 
-    far_first = (4, 3, 5, 2, 6, 1, 7)
+    far_first = (6, 5, 7, 4, 2, 1, 3)
     for k in far_first:
         meet(k).start()
     own_state.start()
     own_truth.start()
 
-    def halo(n, buf, i):
+    def halo(n, buf, part, i):
+        lanes = pl.ds(part * 256, 256)
         dr, dq = AROUND[i]
 
         def cut(step, size, low, high):
@@ -107,10 +111,10 @@
             return pl.ds(1, size) if step == 0 else pl.ds(0 if step > 0 else size + 1, 1)
 
         return send(
-            buf.at[cut(dr, 4, 1, 4), cut(dq, 8, 1, 8)],
-            buf.at[edge(dr, 4), edge(dq, 8)],
-            hsend.at[n, i],
-            hrecv.at[n, i],
+            buf.at[cut(dr, 4, 1, 4), cut(dq, 8, 1, 8), :, lanes],
+            buf.at[edge(dr, 4), edge(dq, 8), :, lanes],
+            hsend.at[n, part, i],
+            hrecv.at[n, part, i],
             near(dr, dq),
         )
 
@@ -120,41 +124,23 @@
             there = ok if there is None else jnp.logical_and(there, ok)
         return there
 
-    def halo_start(n, buf):
+    def halo_start(n, buf, part):
         for i, (dr, dq) in enumerate(AROUND):
             @pl.when(inside(dr, dq))
             def _():
-                halo(n, buf, i).start()
-
-    def halo_sent(n, buf):
+                halo(n, buf, part, i).start()
+
+    def halo_sent(n, buf, part):
         for i, (dr, dq) in enumerate(AROUND):
             @pl.when(inside(dr, dq))
             def _():
-                halo(n, buf, i).wait_send()
-
-    def halo_wait(n, buf):
+                halo(n, buf, part, i).wait_send()
+
+    def halo_wait(n, buf, part):
         for i, (dr, dq) in enumerate(AROUND):
             @pl.when(inside(-dr, -dq))
             def _():
-                halo(n, buf, i).wait_recv()
-
-        @pl.when(rows == 0)
-        def _():
-            buf[0] = jnp.zeros((10, 16, 512), bf)
-
-        @pl.when(rows == 31)
-        def _():
-            buf[5] = jnp.zeros((10, 16, 512), bf)
-
-        @pl.when(q == 0)
-        def _():
-            for r in range(6):
-                buf[r, 0] = jnp.zeros((16, 512), bf)
-
-        @pl.when(q == 7)
-        def _():
-            for r in range(6):
-                buf[r, 9] = jnp.zeros((16, 512), bf)
+                halo(n, buf, part, i).wait_recv()
 
     def view(buf, down, across):
         return buf[pl.ds(down, 4), pl.ds(across, 8)].reshape(512, 512)
@@ -332,6 +318,26 @@
             row = [fin[g, i, tap // 2, :, off : off + 64] for i in range(8)]
             out_ref[g, tap] = jnp.concatenate(row, axis=1)
 
+    for buf in (state, hidden, cots):
+
+        @pl.when(rows == 0)
+        def _():
+            buf[0] = jnp.zeros((10, 16, 512), bf)
+
+        @pl.when(rows == 31)
+        def _():
+            buf[5] = jnp.zeros((10, 16, 512), bf)
+
+        @pl.when(q == 0)
+        def _():
+            for r in range(6):
+                buf[r, 0] = jnp.zeros((16, 512), bf)
+
+        @pl.when(q == 7)
+        def _():
+            for r in range(6):
+                buf[r, 9] = jnp.zeros((16, 512), bf)
+
     own_state.wait()
     for k in range(1, 8):
         meet(k).wait_recv()
@@ -346,40 +352,53 @@
 
     for l in range(4):
         state[1:5, 1:9, :, l * 128 : l * 128 + 128] = base[l].astype(bf).reshape(4, 8, 16, 128)
-    halo_start(0, state)
+    halo_start(0, state, 0)
+    halo_start(0, state, 1)
     load_w1.wait()
-    halo_wait(0, state)
-    state_out.start()
-
-    def conv(buf, w, half):
+
+    def conv(buf, w, half, part):
         total = None
         for tap in range(9):
+            piece = buf[pl.ds(tap // 3, 4), pl.ds(tap % 3, 8), :, part * 256 : part * 256 + 256].reshape(512, 256)
             term = jnp.dot(
-                view(buf, tap // 3, tap % 3), w[tap, :, half * 256 : half * 256 + 256], preferred_element_type=f32
+                piece,
+                w[tap, part * 256 : part * 256 + 256, half * 256 : half * 256 + 256],
+                preferred_element_type=f32,
             )
             total = term if total is None else total + term
         return total
 
+    halo_wait(0, state, 0)
+    for half in range(2):
+        slope[:, half * 256 : half * 256 + 256] = conv(state, w1, half, 0)
+    halo_wait(0, state, 1)
+    state_out.start()
     for half in range(2):
         lanes = slice(half * 256, half * 256 + 256)
-        pre = conv(state, w1, half)
+        pre = slope[:, lanes] + conv(state, w1, half, 1)
         both = 0.5 * (1.0 + lax.erf(pre * INV_ROOT_TWO))
         slope[:, lanes] = both + pre * jnp.exp(-0.5 * pre * pre) * INV_ROOT_TWOPI
         hidden[1:5, 1:9, :, lanes] = (pre * both).astype(bf).reshape(4, 8, 16, 256)
-
-    halo_start(1, hidden)
+        halo_start(1, hidden, half)
+
     load_w2.wait()
-    halo_wait(1, hidden)
-    hidden_out.start()
-    for half in range(2):
-        total = conv(hidden, w2, half)
-        for l in range(2):
-            fore[half * 2 + l] = base[half * 2 + l] + total[:, l * 128 : l * 128 + 128]
+    for part in range(2):
+        halo_wait(1, hidden, part)
+        if part == 1:
+            hidden_out.start()
+        for half in range(2):
+            total = conv(hidden, w2, half, part)
+            for l in range(2):
+                before = (base, fore)[part][half * 2 + l]
+                fore[half * 2 + l] = before + total[:, l * 128 : l * 128 + 128]
 
     for l in range(4):
         for k in range(16):
             value = fore[l, pl.ds(k, 32, stride=16), :]
             leaving[k // 2, (k % 2) * 32 : (k % 2) * 32 + 32, l * 128 : l * 128 + 128] = value.astype(bf)
+
+    for k in (2, 1, 3):
+        leave(k).start()
 
     own_truth.wait()
 
@@ -415,7 +434,8 @@
         cc[:, lanes] = value
         cots[1:5, 1:9, :, lanes] = value.reshape(4, 8, 16, 128)
     cot_out.start()
-    halo_start(2, cots)
+    halo_start(2, cots, 0)
+    halo_start(2, cots, 1)
 
     ct[0] = turned(cc[:, pl.ds(mine, 256)])
     cot_out.wait_recv()
@@ -425,8 +445,9 @@
         form(0, part, hidden, hidden_sib)
     relay1(0, 0)
 
-    halo_wait(2, cots)
-    for k in far_first:
+    halo_wait(2, cots, 0)
+    halo_wait(2, cots, 1)
+    for k in (6, 5, 7, 4):
         leave(k).start()
     prog_ref[q] = leaving[member]
     for half in range(2):
@@ -489,7 +510,8 @@
     for copy in (state_out, hidden_out, cot_out, pre_out):
         copy.wait_send()
     for n, buf in enumerate((state, hidden, cots)):
-        halo_sent(n, buf)
+        halo_sent(n, buf, 0)
+        halo_sent(n, buf, 1)
     for g in range(2):
         for part in range(4):
             for h in range(2):
@@ -539,7 +561,7 @@
         vmem((2, 8, 5, 32, 128), bf),
         vmem((2, 8, 5, 16, 128), bf),
     ]
-    scratch += [dma((4,)), dma((4,)), dma((4,)), dma((3, 8)), dma((3, 8)), dma((2, 8)), dma((2, 8))]
+    scratch += [dma((4,)), dma((4,)), dma((4,)), dma((3, 2, 8)), dma((3, 2, 8)), dma((2, 8)), dma((2, 8))]
     for dims in ((2, 16, 3), (2, 8, 4), (2, 4, 8), (2, 2, 8)):
         scratch += [dma(dims), dma(dims)]
     in_vmem = pl.BlockSpec(memory_space=pltpu.VMEM)
@@ -560,8 +582,8 @@
         state, truth, jnp.transpose(conv_first, (1, 0, 2)), jnp.transpose(conv_second, (1, 0, 2))
     )
     prognosis = prognosis.reshape(8, members, rows, cols // 8, channels).transpose(1, 2, 0, 3, 4).reshape(state.shape)
-    slopes = jnp.transpose(slopes.astype(jnp.float32), (0, 2, 1, 3))
-    return prognosis, slopes[1], slopes[0]
+    second, first = [jnp.transpose(slopes[g], (1, 0, 2)).astype(jnp.float32) for g in range(2)]
+    return prognosis, first, second
 
 
 def solution(mesh):

time: 117 us -> 115 us (0.983)
  Pallas kernels: 113 us -> 111 us
    pallas_call x1, Pallas kernels: 113 us -> 111 us  [whole_step(): pl.pallas_call(step_kernel, out_shape=[jax.ShapeDtypeStruct((8, 64, 512),...]
    convert_element_type x0 -> x1, other arithmetic: none -> 1.86 us  [body(): jnp.transpose(slopes[g], (1, 0, 2)).astype(jnp.float32)]
where the time goes in v7:
time: 115 us
  Pallas kernels  111 us (97%)
  local copies, waits for them, and re-layouts  1.88 us (2%)
  other arithmetic  1.86 us (2%)
    pallas_call x1, Pallas kernels, whole_step(): pl.pallas_call(step_kernel, out_shape=[jax.ShapeDtypeStruct((8, 64, 512),...  111 us

profile of v7, /device:TPU:1, one launch (start us, length us, event | category | flops | bytes accessed | tf_op | source)
XLA Modules:
  0.0 114.9 jit_solution(9639695647809348552)
XLA Ops:
  0.6 110.5 %whole_step.1 = (bf16[8,64,512]{2,1,0:T(8,128)(2,1)}, bf16[2,9,16,512]{3,2,1,0:T(8,128)(2,1)}) custom-call(bf16[2,4,64,512]{3,2,1,0:T(8,128)(2,1)} %state_hbm.1, bf16[4,64,512]{2,1,0:T(8,128)(2,1)} %truth_hbm.1, bf16[9,512,512]{2,1,0:T(8,128)(2,1)} %bitcast.18, bf16[9,512,512]{2,1,0:T(8,128)(2,1)} %bitcast.19), custom_call_target="tpu_custom_call" | custom-call | tf_op jit(solution)/shard_map/whole_step/pallas_call | solution.py:568
  111.1 1.9 %copy.9 = bf16[2,4,8,8,512]{4,3,2,1,0:T(8,128)(2,1)} copy(bf16[2,4,8,8,512]{4,3,1,0,2:T(8,128)(2,1)} %bitcast.21) | data formatting | bytes 1048576 | tf_op jit(solution)/shard_map/transpose | solution.py:584
  113.0 1.9 %convert_bitcast_fusion = (f32[16,9,512]{2,0,1:T(8,128)}, f32[16,9,512]{2,0,1:T(8,128)}) fusion(bf16[2,9,16,512]{3,2,1,0:T(8,128)(2,1)} %get-tuple-element.6), kind=kLoop, calls=%fused_computation.1 | loop fusion | flops 147456 | bytes 884736 | tf_op jit(solution)/shard_map/convert_element_type | solution.py:585

commit v8 on v7

--- a/solution.py
+++ b/solution.py
@@ -101,7 +101,7 @@
     own_truth.start()
 
     def halo(n, buf, part, i):
-        lanes = pl.ds(part * 256, 256)
+        lanes = pl.ds(pl.multiple_of(part * 256, 256) if not isinstance(part, int) else part * 256, 256)
         dr, dq = AROUND[i]
 
         def cut(step, size, low, high):
@@ -402,40 +402,42 @@
 
     own_truth.wait()
 
-    @pl.loop(0, 4)
-    def _(l):
-        @pl.loop(0, 4)
-        def _(cell):
-            fact = truth[cell, :, pl.ds(pl.multiple_of(l * 128, 128), 128)].astype(f32)
-
-            def spot_of(k):
-                return pl.ds(cell * 128 + k, 8, stride=16)
-
-            xs = [fore[l, spot_of(k), :] for k in range(16)]
-            pulls = [None] * 16
-
-            def plus(i, v):
-                pulls[i] = v if pulls[i] is None else pulls[i] + v
-
-            for a in range(16):
-                for b in range(a + 1, 16):
-                    d = xs[a] - xs[b]
-                    u = d * lax.rsqrt(d * d + EPS2)
-                    plus(a, u)
-                    plus(b, -u)
-            for k in range(16):
-                d = xs[k] - fact
-                away = d * lax.rsqrt(d * d + EPS2)
-                fore[l, spot_of(k), :] = away * (1.0 / 2048.0) - pulls[k] * (1.0 / 30720.0)
-
-    for l in range(4):
-        lanes = slice(l * 128, l * 128 + 128)
-        value = fore[l].astype(bf)
-        cc[:, lanes] = value
-        cots[1:5, 1:9, :, lanes] = value.reshape(4, 8, 16, 128)
-    cot_out.start()
-    halo_start(2, cots, 0)
-    halo_start(2, cots, 1)
+    for part, to_sibling in ((1 - c, True), (c, False)):
+
+        @pl.loop(part * 2, part * 2 + 2)
+        def _(l):
+            @pl.loop(0, 4)
+            def _(cell):
+                fact = truth[cell, :, pl.ds(pl.multiple_of(l * 128, 128), 128)].astype(f32)
+
+                def spot_of(k):
+                    return pl.ds(cell * 128 + k, 8, stride=16)
+
+                xs = [fore[l, spot_of(k), :] for k in range(16)]
+                pulls = [None] * 16
+
+                def plus(i, v):
+                    pulls[i] = v if pulls[i] is None else pulls[i] + v
+
+                for a in range(16):
+                    for b in range(a + 1, 16):
+                        d = xs[a] - xs[b]
+                        u = d * lax.rsqrt(d * d + EPS2)
+                        plus(a, u)
+                        plus(b, -u)
+                for k in range(16):
+                    d = xs[k] - fact
+                    away = d * lax.rsqrt(d * d + EPS2)
+                    fore[l, spot_of(k), :] = away * (1.0 / 2048.0) - pulls[k] * (1.0 / 30720.0)
+
+        for i in range(2):
+            lanes = pl.ds(pl.multiple_of(part * 256 + i * 128, 128), 128)
+            value = fore[part * 2 + i].astype(bf)
+            cc[:, lanes] = value
+            cots[1:5, 1:9, :, lanes] = value.reshape(4, 8, 16, 128)
+        if to_sibling:
+            cot_out.start()
+        halo_start(2, cots, part)
 
     ct[0] = turned(cc[:, pl.ds(mine, 256)])
     cot_out.wait_recv()
@@ -445,27 +447,36 @@
         form(0, part, hidden, hidden_sib)
     relay1(0, 0)
 
+    def adjoint(i_lanes, part):
+        total = None
+        for tap in range(9):
+            down, across = 2 - tap // 3, 2 - tap % 3
+            o_lanes = slice(part * 256, part * 256 + 256)
+            piece = cots[down : down + 4, across : across + 8, :, o_lanes].reshape(512, 256)
+            term = lax.dot_general(
+                piece, w2[tap, i_lanes, o_lanes], (((1,), (1,)), ((), ())), preferred_element_type=f32
+            )
+            total = term if total is None else total + term
+        return total
+
     halo_wait(2, cots, 0)
+    for i, start in enumerate((theirs, mine)):
+        total = adjoint(pl.ds(start, 256), 0)
+        for l in range(2):
+            base[i * 2 + l] = total[:, l * 128 : l * 128 + 128]
     halo_wait(2, cots, 1)
+    for i, start in enumerate((theirs, mine)):
+        total = jnp.concatenate([base[i * 2], base[i * 2 + 1]], axis=1) + adjoint(pl.ds(start, 256), 1)
+        cp[:, pl.ds(start, 256)] = (total * slope[:, pl.ds(start, 256)]).astype(bf)
+        if i == 0:
+            pre_out.start()
+            relay1(0, 1)
     for k in (6, 5, 7, 4):
         leave(k).start()
     prog_ref[q] = leaving[member]
-    for half in range(2):
-        lanes = pl.ds(half * 256, 256)
-        total = None
-        for tap in range(9):
-            term = lax.dot_general(
-                view(cots, 2 - tap // 3, 2 - tap % 3),
-                w2[tap, lanes],
-                (((1,), (1,)), ((), ())),
-                preferred_element_type=f32,
-            )
-            total = term if total is None else total + term
-        cp[:, lanes] = (total * slope[:, lanes]).astype(bf)
-        for part in ((1, 2), (3,))[half]:
-            relay1(0, part)
-
-    pre_out.start()
+    relay1(0, 2)
+    relay1(0, 3)
+
     ct[0] = turned(cp[:, pl.ds(mine, 256)])
     add1(0, 0)
     pre_out.wait_recv()

time: 115 us -> 115 us (level)
  no operation moved by 1% of the time
where the time goes in v8:
time: 115 us
  Pallas kernels  110 us (96%)
  local copies, waits for them, and re-layouts  1.88 us (2%)
  other arithmetic  1.86 us (2%)
    pallas_call x1, Pallas kernels, whole_step(): pl.pallas_call(step_kernel, out_shape=[jax.ShapeDtypeStruct((8, 64, 512),...  110 us

profile of v8, /device:TPU:1, one launch (start us, length us, event | category | flops | bytes accessed | tf_op | source)
XLA Modules:
  0.0 114.6 jit_solution(16884984616577798030)
XLA Ops:
  0.6 110.2 %whole_step.1 = (bf16[8,64,512]{2,1,0:T(8,128)(2,1)}, bf16[2,9,16,512]{3,2,1,0:T(8,128)(2,1)}) custom-call(bf16[2,4,64,512]{3,2,1,0:T(8,128)(2,1)} %state_hbm.1, bf16[4,64,512]{2,1,0:T(8,128)(2,1)} %truth_hbm.1, bf16[9,512,512]{2,1,0:T(8,128)(2,1)} %bitcast.18, bf16[9,512,512]{2,1,0:T(8,128)(2,1)} %bitcast.19), custom_call_target="tpu_custom_call" | custom-call | tf_op jit(solution)/shard_map/whole_step/pallas_call | solution.py:579
  110.9 1.9 %copy.9 = bf16[2,4,8,8,512]{4,3,2,1,0:T(8,128)(2,1)} copy(bf16[2,4,8,8,512]{4,3,1,0,2:T(8,128)(2,1)} %bitcast.21) | data formatting | bytes 1048576 | tf_op jit(solution)/shard_map/transpose | solution.py:595
  112.8 1.9 %convert_bitcast_fusion = (f32[16,9,512]{2,0,1:T(8,128)}, f32[16,9,512]{2,0,1:T(8,128)}) fusion(bf16[2,9,16,512]{3,2,1,0:T(8,128)(2,1)} %get-tuple-element.6), kind=kLoop, calls=%fused_computation.1 | loop fusion | flops 147456 | bytes 884736 | tf_op jit(solution)/shard_map/convert_element_type | solution.py:596

commit v9 on v8

--- a/solution.py
+++ b/solution.py
@@ -496,12 +496,12 @@
     relay1(1, 2)
     relay1(1, 3)
     add1(1, 0)
+    add1(1, 1)
+    add2(1, 0)
     for part in range(4):
         add3(0, part)
     spread(0, 0)
     spread(0, 1)
-    add1(1, 1)
-    add2(1, 0)
     add1(1, 2)
     add2(1, 1)
     add1(1, 3)

time: 115 us -> 113 us (0.983)
  Pallas kernels: 110 us -> 108 us
    pallas_call x1, Pallas kernels: 110 us -> 108 us  [whole_step(): pl.pallas_call(step_kernel, out_shape=[jax.ShapeDtypeStruct((8, 64, 512),...]
where the time goes in v9:
time: 113 us
  Pallas kernels  108 us (96%)
  local copies, waits for them, and re-layouts  1.88 us (2%)
  other arithmetic  1.86 us (2%)
    pallas_call x1, Pallas kernels, whole_step(): pl.pallas_call(step_kernel, out_shape=[jax.ShapeDtypeStruct((8, 64, 512),...  108 us

profile of v9, /device:TPU:1, one launch (start us, length us, event | category | flops | bytes accessed | tf_op | source)
XLA Modules:
  0.0 112.9 jit_solution(6790399410268135179)
XLA Ops:
  0.6 108.5 %whole_step.1 = (bf16[8,64,512]{2,1,0:T(8,128)(2,1)}, bf16[2,9,16,512]{3,2,1,0:T(8,128)(2,1)}) custom-call(bf16[2,4,64,512]{3,2,1,0:T(8,128)(2,1)} %state_hbm.1, bf16[4,64,512]{2,1,0:T(8,128)(2,1)} %truth_hbm.1, bf16[9,512,512]{2,1,0:T(8,128)(2,1)} %bitcast.18, bf16[9,512,512]{2,1,0:T(8,128)(2,1)} %bitcast.19), custom_call_target="tpu_custom_call" | custom-call | tf_op jit(solution)/shard_map/whole_step/pallas_call | solution.py:579
  109.1 1.9 %copy.9 = bf16[2,4,8,8,512]{4,3,2,1,0:T(8,128)(2,1)} copy(bf16[2,4,8,8,512]{4,3,1,0,2:T(8,128)(2,1)} %bitcast.21) | data formatting | bytes 1048576 | tf_op jit(solution)/shard_map/transpose | solution.py:595
  111.0 1.9 %convert_bitcast_fusion = (f32[16,9,512]{2,0,1:T(8,128)}, f32[16,9,512]{2,0,1:T(8,128)}) fusion(bf16[2,9,16,512]{3,2,1,0:T(8,128)(2,1)} %get-tuple-element.6), kind=kLoop, calls=%fused_computation.1 | loop fusion | flops 147456 | bytes 884736 | tf_op jit(solution)/shard_map/convert_element_type | solution.py:596
